TPU v7x, 128 devices: a whole 4x4x4 slice. The times are simulated.
128 devices in a mesh: row: 16 (over z, x), col: 8 (over y, core).
Axes of the slice: x: 4, y: 4, z: 4, core: 2. Of those that a mesh axis runs over, the one named last changes fastest.
Arguments:
- slab: float32 [2048, 131072], P('col', 'row'), may hold values from -6 to 6
- stored: float32 [128, 131072], P(('row', 'col')), may hold values from -6 to 6
- owner: int32 [4], replicated, may hold values from 0 to 127
Outputs:
- result: float32 [2048, 131072], P('col', 'row')
All inputs are finite; a program needn't handle non-finite values.
Results may differ from a plain program's by a relative error of at most 0.0001.
Values sent between devices are 32-bit elements; how exact they have to be, the bound alone decides.
A program may use at most 192 MiB of HBM per device.

v0:
```python
import jax
import jax.numpy as jnp
from jax import lax
from jax.sharding import PartitionSpec as P

BAND = 64
GROUPS = 4


def from_root(block, axis, owner):
    block = jnp.where(lax.axis_index(axis) == owner, block, jnp.zeros_like(block))
    return lax.psum(block, axis)


def offset_of(group):
    return 1 + (37 * group + 11) % 63


def fetch_vector(stored, owner, group):
    return from_root(stored, ("row", "col"), owner[group])[0]


def window_scales(vector, start, count):
    vwin = lax.slice_in_dim(vector, start, start + (count - 1) * BAND, axis=0).reshape(
        count - 1, BAND
    )
    return (vwin, 2.0 / (jnp.sum(vwin * vwin, axis=-1) + 1e-06))


def lane_table(start):
    lane_index = jnp.arange(2 * BAND)
    half_index = lane_index // BAND
    tail_flag = (lane_index % BAND >= start).astype(jnp.int32)
    column_index = 2 * half_index + tail_flag
    return (column_index[:, None] == jnp.arange(4)[None, :]).astype(jnp.float32)


def head_tail(values, vector_flat, selector):
    rows_count, length = values.shape
    product = (values * vector_flat[None]).reshape(rows_count, length // (2 * BAND), 2 * BAND)
    sums = jnp.dot(
        product, selector, precision=lax.Precision.HIGHEST, preferred_element_type=jnp.float32
    )
    sums = sums.reshape(rows_count, length // BAND, 2)
    return (sums[:, :, 0], sums[:, :, 1])


def apply_coef(values, vector_flat, before, own, selector):
    rows_count, length = values.shape
    coefs = jnp.stack([before, own], axis=-1).reshape(rows_count, length // (2 * BAND), 4)
    lane_values = jnp.dot(
        coefs, selector.T, precision=lax.Precision.HIGHEST, preferred_element_type=jnp.float32
    )
    return values - lane_values.reshape(rows_count, length) * vector_flat[None]


def shards(slab, stored, owner):
    parts = lax.axis_size("row")
    columns, rows_dev = slab.shape
    tiles_dev = rows_dev // BAND
    order = rows_dev * parts
    count = order // BAND
    gathered = lax.all_to_all(slab, "row", split_axis=0, concat_axis=1, tiled=True)
    owned = gathered.shape[0]
    zero_col = jnp.zeros((owned, 1), jnp.float32)
    for group in range(GROUPS):
        start = offset_of(group)
        vector = fetch_vector(stored, owner, group)
        vwin, tau = window_scales(vector, start, count)
        tau_full = jnp.concatenate([tau, jnp.zeros((1,), jnp.float32)])
        v_slab = vector.reshape(tiles_dev, parts, BAND).transpose(1, 0, 2).reshape(order)
        selector = lane_table(start)
        head, tail = head_tail(gathered, v_slab, selector)
        head_nat = head.reshape(owned, parts, tiles_dev).transpose(0, 2, 1).reshape(owned, count)
        tail_nat = tail.reshape(owned, parts, tiles_dev).transpose(0, 2, 1).reshape(owned, count)
        scaled = (tail_nat + jnp.concatenate([head_nat[:, 1:], zero_col], axis=1)) * tau_full[None]
        before = jnp.concatenate([zero_col, scaled[:, :-1]], axis=1)
        scaled_slab = (
            scaled.reshape(owned, tiles_dev, parts).transpose(0, 2, 1).reshape(owned, count)
        )
        before_slab = (
            before.reshape(owned, tiles_dev, parts).transpose(0, 2, 1).reshape(owned, count)
        )
        gathered = apply_coef(gathered, v_slab, before_slab, scaled_slab, selector)
    return lax.all_to_all(gathered, "row", split_axis=1, concat_axis=0, tiled=True)


def solution(mesh):
    placed = (P("col", "row"), P(("row", "col"), None), P())
    return jax.shard_map(
        shards, mesh=mesh, in_specs=placed, out_specs=P("col", "row"), check_vma=False
    )
```

profile of v0, /device:TPU:0, one launch (start us, length us, event | category | flops | bytes accessed | tf_op | source)
XLA Modules:
  0.0 652.5 jit_solution(16296625976132326592)
XLA Ops:
  6.5 8.2 %all-to-all-start = ((f32[16,16,8192]{2,1,0:T(8,128)}), f32[16,16,8192]{2,1,0:T(8,128)}, u32[]{:S(2)}, u32[]{:S(2)}) async-start(f32[16,16,8192]{2,1,0:T(8,128)} %bitcast.93), calls=%async_computation | async-start | bytes 16777216 | tf_op jit(solution)/shard_map/all_to_all | solution.py:63
  17.8 2.7 broadcast_select_fusion
  20.6 239.9 %all-reduce.11.cloned.1.call-done = (f32[1,131072]{1,0:T(1,128)}, f32[1,131072]{1,0:T(1,128)}, f32[1,131072]{1,0:T(1,128)}, f32[1,131072]{1,0:T(1,128)}) async-done(((f32[1,131072]{1,0:T(1,128)}, f32[1,131072]{1,0:T(1,128)}, f32[1,131072]{1,0:T(1,128)}, f32[1,131072]{1,0:T(1,128)}), (f32[1,131072]{1,0:T(1,128)}, f32[1,131072]{1,0:T(1,128)}, f32[1,131072]{1,0:T(1,128)}, ...) | async-done | bytes 2097168 | tf_op jit(solution)/shard_map/psum | solution.py:12
  261.0 2.9 reduce.28
  265.9 2.9 reduce.29
  270.7 2.9 reduce.31
  276.4 2.9 reduce.30
  281.3 5.0 fusion.21
  287.6 5.0 fusion.19
  292.6 2.2 mul.250
  295.1 1.6 reduce_sum.39
  299.2 12.0 %copy.56 = f32[16,16,8192]{2,1,0:T(8,128)} copy(f32[16,16,8192]{2,0,1:T(8,128)} %bitcast.1) | data formatting | bytes 16777216 | tf_op jit(solution)/shard_map/all_to_all | solution.py:63
  311.2 9.3 %all_to_all.29 = f32[16,1024,128]{2,1,0:T(8,128)} reshape(f32[16,16,8192]{2,1,0:T(8,128)} %copy.56) | data formatting | bytes 16777216 | tf_op jit(solution)/shard_map/all_to_all | solution.py:63
  320.5 7.5 %fusion.12 = f32[16,1024,4]{1,2,0:T(4,128)S(1)} fusion(f32[16,1024,128]{2,1,0:T(8,128)} %all_to_all.29, f32[1024,128]{1,0:T(8,128)S(1)} %mul.212, s32[128]{0:T(128)S(1)} %fusion.48), kind=kOutput, calls=%fused_computation.18 | convolution fusion | flops 102760960 | bytes 9175552 | tf_op jit(solution)/shard_map/dot_general | solution.py:41
  328.0 1.7 copy.58
  329.7 4.9 fusion.55
  334.7 2.2 copy.62
  337.6 2.2 copy.60
  342.2 1.5 copy.63
  344.2 2.2 copy.65
  346.4 1.9 copy.66
  348.3 9.1 %fusion.36 = f32[16,1024,128]{2,1,0:T(8,128)} fusion(f32[16,1024,4]{1,2,0:T(4,128)S(1)} %copy.66, s32[128]{0:T(128)S(1)} %fusion.48), kind=kOutput, calls=%fused_computation.70 | convolution fusion | flops 100663808 | bytes 8651264 | tf_op jit(solution)/shard_map/dot_general | solution.py:51
  357.4 9.4 %reshape.241 = f32[16,16,8192]{2,1,0:T(8,128)} reshape(f32[16,1024,128]{2,1,0:T(8,128)} %fusion.36) | data formatting | bytes 16777216 | tf_op jit(solution)/shard_map/reshape | solution.py:54
  366.8 10.5 %fusion.10 = f32[16,1024,4]{1,2,0:T(4,128)S(1)} fusion(f32[1024,128]{1,0:T(8,128)S(1)} %mul.224, f32[16,1024,128]{2,1,0:T(8,128)} %all_to_all.29, f32[16,1024,128]{2,1,0:T(8,128)} %fusion.36, f32[1024,128]{1,0:T(8,128)S(1)} %mul.212, s32[128]{0:T(128)S(1)} %fusion.49), kind=kOutput, calls=%fused_computation.15 | convolution fusion | flops 106955264 | bytes 18088448 | tf_op jit(solution)/shard_map/dot_general | solution.py:41
  377.3 1.8 copy.70
  379.1 5.2 fusion.54
  384.3 2.2 copy.74
  387.2 2.2 copy.72
  390.5 1.4 reshape.245
  391.9 1.5 copy.75
  393.8 2.3 copy.77
  396.1 1.9 copy.78
  398.0 13.9 %multiply_subtract_fusion = (f32[16,1024,128]{2,1,0:T(8,128)}, f32[16,1024,128]{2,1,0:T(8,128)}) fusion(f32[1024,128]{1,0:T(8,128)S(1)} %mul.224, f32[16,1024,128]{2,1,0:T(8,128)} %all_to_all.29, f32[16,1024,128]{2,1,0:T(8,128)} %fusion.36, f32[1024,128]{1,0:T(8,128)S(1)} %mul.212, f32[16,1024,4]{1,2,0:T(4,128)S(1)} %copy.78, s32[128]{0:T(128)S(1)} %fusion.49), kind=kOutput, calls=%fused_computation.14 | convolution fusion | flops 109052416 | bytes 34865664 | tf_op jit(solution)/shard_map/dot_general | solution.py:51
  411.9 9.8 %reshape.248 = f32[16,16,8192]{2,1,0:T(8,128)} reshape(f32[16,1024,128]{2,1,0:T(8,128)} %get-tuple-element.26) | data formatting | bytes 16777216 | tf_op jit(solution)/shard_map/reshape | solution.py:54
  421.7 7.5 %fusion.8 = f32[16,1024,4]{1,2,0:T(4,128)S(1)} fusion(f32[16,1024,128]{2,1,0:T(8,128)} %get-tuple-element.25, f32[1024,128]{1,0:T(8,128)S(1)} %mul.235, s32[128]{0:T(128)S(1)} %fusion.50), kind=kOutput, calls=%fused_computation.12 | convolution fusion | flops 102760960 | bytes 9175552 | tf_op jit(solution)/shard_map/dot_general | solution.py:41
  430.1 2.7 fusion.53
  432.8 2.2 copy.86
  435.7 2.2 copy.84
  441.9 9.0 %fusion.30 = f32[16,1024,128]{2,1,0:T(8,128)} fusion(f32[16,1024,4]{1,2,0:T(4,128)S(1)} %copy.90, s32[128]{0:T(128)S(1)} %fusion.50), kind=kOutput, calls=%fused_computation.68 | convolution fusion | flops 100663808 | bytes 8651264 | tf_op jit(solution)/shard_map/dot_general | solution.py:51
  450.9 9.4 %reshape.255 = f32[16,16,8192]{2,1,0:T(8,128)} reshape(f32[16,1024,128]{2,1,0:T(8,128)} %fusion.30) | data formatting | bytes 16777216 | tf_op jit(solution)/shard_map/reshape | solution.py:54
  460.4 10.5 %fusion.4 = f32[16,1024,4]{1,2,0:T(4,128)S(1)} fusion(f32[16,1024,128]{2,1,0:T(8,128)} %get-tuple-element.25, f32[16,1024,128]{2,1,0:T(8,128)} %fusion.30, f32[1024,128]{1,0:T(8,128)S(1)} %copy-done.4, f32[1024,128]{1,0:T(8,128)S(1)} %mul.235, s32[128]{0:T(128)S(1)} %fusion.51), kind=kOutput, calls=%fused_computation.8 | convolution fusion | flops 106955264 | bytes 18088448 | tf_op jit(solution)/shard_map/dot_general | solution.py:41
  471.8 2.6 fusion.52
  474.4 2.2 copy.98
  482.5 8.9 %fusion.27 = f32[16,1024,128]{2,1,0:T(8,128)} fusion(f32[16,1024,4]{1,2,0:T(4,128)S(1)} %copy.102, s32[128]{0:T(128)S(1)} %fusion.51), kind=kOutput, calls=%fused_computation.67 | convolution fusion | flops 100663808 | bytes 8651264 | tf_op jit(solution)/shard_map/dot_general | solution.py:51
  491.5 9.5 %reshape.262 = f32[16,16,8192]{2,1,0:T(8,128)} reshape(f32[16,1024,128]{2,1,0:T(8,128)} %fusion.27) | data formatting | bytes 16777216 | tf_op jit(solution)/shard_map/reshape | solution.py:54
  501.0 39.5 %fusion = f32[16,16,8192]{2,0,1:T(8,128)} fusion(f32[16,16,8192]{2,1,0:T(8,128)} %reshape.262, f32[16,16,8192]{2,1,0:T(8,128)} %reshape.255, f32[16,16,8192]{2,1,0:T(8,128)} %reshape.248, f32[16,16,8192]{2,1,0:T(8,128)} %reshape.241, f32[16,8192]{1,0:T(8,128)S(1)} %copy-done.2, f32[16,8192]{1,0:T(8,128)S(1)} %copy-done.3, f32[16,8192]{1,0:T(8,128)S(1)} %copy-done, ...), kind=kLoop, calls=%fused_computation.1 | loop fusion | flops 16777216 | bytes 52428800 | tf_op jit(solution)/shard_map/sub | solution.py:54
  540.5 101.3 %all_to_all.35 = f32[16,16,8192]{2,0,1:T(8,128)S(1)} all-to-all(f32[16,16,8192]{2,0,1:T(8,128)} %fusion), channel_id=1, replica_groups=mesh['row'=16,'col'=8] {'row'}, dimensions={1} | all-to-all | bytes 16777216 | tf_op jit(solution)/shard_map/all_to_all | solution.py:85
  641.9 3.4 copy.144
  (105 shorter events, 31.7 us)
Async XLA Ops:
  6.5 8.2 %copy-start.6 = (s32[4]{0:T(128)S(1)}, s32[4]{0:T(128)}, u32[]{:S(2)}) copy-start(s32[4]{0:T(128)} %param.5) | copy-start | bytes 52
  6.5 11.3 %copy-start.5 = (f32[1,131072]{1,0:T(1,128)S(1)}, f32[1,131072]{1,0:T(1,128)}, u32[]{:S(2)}) copy-start(f32[1,131072]{1,0:T(1,128)} %param.4) | copy-start | bytes 1572868
  6.5 292.7 %all-to-all-start = ((f32[16,16,8192]{2,1,0:T(8,128)}), f32[16,16,8192]{2,1,0:T(8,128)}, u32[]{:S(2)}, u32[]{:S(2)}) async-start(f32[16,16,8192]{2,1,0:T(8,128)} %bitcast.93), calls=%async_computation | async-start | bytes 16777216 | tf_op jit(solution)/shard_map/all_to_all | solution.py:63
  14.7 245.8 %all-reduce.11.cloned.1.call-start = ((), (), s32[]{:S(2)}) async-start(), calls=%async_computation.2 | async-start | bytes 4194304 | tf_op jit(solution)/shard_map/psum | solution.py:12
  450.9 9.5 %copy-start.4 = (f32[1024,128]{1,0:T(8,128)S(1)}, f32[1024,128]{1,0:T(8,128)}, u32[]{:S(2)}) copy-start(f32[1024,128]{1,0:T(8,128)} %mul.246) | copy-start | bytes 1572868
  491.4 9.5 %copy-start = (f32[16,8192]{1,0:T(8,128)S(1)}, f32[16,8192]{1,0:T(8,128)}, u32[]{:S(2)}) copy-start(f32[16,8192]{1,0:T(8,128)} %mul.231) | copy-start | bytes 1572868
  491.4 9.5 %copy-start.1 = (f32[16,8192]{1,0:T(8,128)S(1)}, f32[16,8192]{1,0:T(8,128)}, u32[]{:S(2)}) copy-start(f32[16,8192]{1,0:T(8,128)} %mul.220) | copy-start | bytes 1572868
  491.4 9.5 %copy-start.2 = (f32[16,8192]{1,0:T(8,128)S(1)}, f32[16,8192]{1,0:T(8,128)}, u32[]{:S(2)}) copy-start(f32[16,8192]{1,0:T(8,128)} %mul.253) | copy-start | bytes 1572868
  491.5 9.5 %copy-start.3 = (f32[16,8192]{1,0:T(8,128)S(1)}, f32[16,8192]{1,0:T(8,128)}, u32[]{:S(2)}) copy-start(f32[16,8192]{1,0:T(8,128)} %mul.242) | copy-start | bytes 1572868
Sparse Core Ops, SparseCore 0:
  21.0 239.4 all-reduce.10
where the time goes:
time: 664 us; the launch traced here: 653 us
  waiting for transfers between devices  240 us (36%)
  local copies, waits for them, and re-layouts  142 us (21%)
  blocking collectives  101 us (15%)
  matrix products  77 us (12%)
  other arithmetic  67.1 us (10%)
  between operations  16.9 us (3%)
  starting transfers between devices  8.21 us (1%)
    psum x1, waiting for transfers between devices, from_root(): return lax.psum(block, axis)  240 us
    all_to_all x1, blocking collectives, shards(): lax.all_to_all(gathered, 'row', split_axis=1, concat_axis=0, tiled=True)  101 us
    dot_general x4, matrix products, apply_coef(): jnp.dot(coefs, selector.T, precision=lax.Precision.HIGHEST, preferred_ele...  41 us
    sub x1, other arithmetic, apply_coef(): return values - lane_values.reshape(rows_count, length) * vector_flat[None]  39.5 us
    reshape x4, local copies, waits for them, and re-layouts, apply_coef(): return values - lane_values.reshape(rows_count, length) * vector_flat[None]  38.1 us
    dot_general x4, matrix products, head_tail(): jnp.dot(product, selector, precision=lax.Precision.HIGHEST, preferred_ele...  36.1 us
    all_to_all x2, local copies, waits for them, and re-layouts, shards(): lax.all_to_all(slab, 'row', split_axis=0, concat_axis=1, tiled=True)  21.3 us
    slice x4, local copies, waits for them, and re-layouts, head_tail(): return (sums[:, :, 0], sums[:, :, 1])  15.5 us
  transfers between devices with their start and end apart: 2, of which 1 were waited for; matrix products, arithmetic and copies ran while one was open for 6% of the time, Pallas kernels for 0%

commit v1 on v0

v1 whole, which is shorter than its diff:
```python
import functools

import jax
import jax.numpy as jnp
from jax import lax
from jax.experimental import pallas as pl
from jax.experimental.pallas import tpu as pltpu
from jax.sharding import PartitionSpec as P

BAND = 64
GROUPS = 4
LANES = 128
CHUNKS = 8
WIDE = CHUNKS * LANES
MESH = pl.DeviceIdType.MESH
F32 = jnp.float32
BF16 = jnp.bfloat16


def offset_of(group):
    return 1 + (37 * group + 11) % 63


def segment(group, side):
    return (0, offset_of(group)) if side == 0 else (offset_of(group), BAND)


PAIRS = []
for _g in range(GROUPS):
    for _s in range(2):
        for _h in range(_g):
            for _t in range(2):
                _lo = max(segment(_g, _s)[0], segment(_h, _t)[0])
                _hi = min(segment(_g, _s)[1], segment(_h, _t)[1])
                if _lo < _hi:
                    PAIRS.append((_g, _s, _h, _t, _lo, _hi))


def split(x):
    high = x.astype(BF16)
    return high, (x - high.astype(F32)).astype(BF16)


def spread(vectors):
    lane = lax.broadcasted_iota(jnp.int32, (CHUNKS, WIDE), 1)
    row = lax.broadcasted_iota(jnp.int32, (CHUNKS, WIDE), 0)
    here = (lane // LANES) == row
    within = lane % LANES
    zero = jnp.zeros((CHUNKS, WIDE), F32)
    highs, lows = [], []
    for g in range(GROUPS):
        v = vectors[g]
        high = v.astype(BF16).astype(F32)
        wide_high = jnp.concatenate([high] * CHUNKS, axis=1)
        wide_low = jnp.concatenate([v - high] * CHUNKS, axis=1)
        for s in range(2):
            lo, hi = segment(g, s)
            masks = [
                here & (within >= BAND * par + lo) & (within < BAND * par + hi) for par in range(2)
            ]
            for wide, into in ((wide_high, highs), (wide_low, lows)):
                both = jnp.concatenate([jnp.where(m, wide, zero) for m in masks], axis=0)
                into.append(both.astype(BF16))
    return jnp.concatenate(highs, axis=0), jnp.concatenate(lows, axis=0)


def contract_lanes(a, b):
    return lax.dot_general(a, b, (((1,), (1,)), ((), ())), preferred_element_type=F32)


def coef_kernel(
    parts, cols, owner_ref, stored_ref, slab_ref, coef_ref, vec_ref,
    row_in, slab_in, high_in, low_in, send1, recv1, send2, recv2, recv3,
    raw, square_out, square_in, gram, tau, send4, recv4,
    row_sem, slab_sem, s1, r1, s2, r2, s3, r3, st, rt, s4, r4,
):
    half = cols * CHUNKS
    me = lax.axis_index("row")
    col = lax.axis_index("col")
    left = lax.rem(me + parts - 1, parts)
    right = lax.rem(me + 1, parts)

    row_copy = pltpu.make_async_copy(stored_ref, row_in, row_sem)
    row_copy.start()

    def slab_copy(b):
        return pltpu.make_async_copy(
            slab_ref.at[:, pl.ds(pl.multiple_of(b * WIDE, WIDE), WIDE)], slab_in.at[b], slab_sem.at[b]
        )

    lax.fori_loop(0, cols, lambda b, _: (slab_copy(b).start(), 0)[1], 0)

    row_copy.wait()
    low_lanes = lax.broadcasted_iota(jnp.int32, (half, LANES), 1) < BAND
    for q in range(parts // 2):
        even = row_in[pl.ds(q, half, stride=parts), :]
        odd = row_in[pl.ds(q + parts // 2, half, stride=parts), :]
        send1[2 * q] = jnp.where(low_lanes, even, pltpu.roll(odd, BAND, 1))
        send1[2 * q + 1] = jnp.where(low_lanes, pltpu.roll(even, BAND, 1), odd)
    recv1[me] = send1[me]

    def copy1(to, source):
        return pltpu.make_async_remote_copy(
            src_ref=send1.at[to], dst_ref=recv1.at[source], send_sem=s1.at[to], recv_sem=r1.at[source],
            device_id={"row": to}, device_id_type=MESH,
        )

    def copy2(to, source):
        return pltpu.make_async_remote_copy(
            src_ref=send2.at[to], dst_ref=recv2.at[source], send_sem=s2.at[to], recv_sem=r2.at[source],
            device_id={"col": to}, device_id_type=MESH,
        )

    def copy3(to, source):
        return pltpu.make_async_remote_copy(
            src_ref=recv3.at[source], dst_ref=recv3.at[source], send_sem=s3.at[to], recv_sem=r3.at[source],
            device_id={"col": to}, device_id_type=MESH,
        )

    def others(size, mine, step):
        def body(r, _):
            step(lax.rem(mine + r, size))
            return 0

        lax.fori_loop(1, size, body, 0)

    others(parts, me, lambda to: copy1(to, me).start())

    rows = slab_in.shape[1]

    def split_block(b, _):
        slab_copy(b).wait()

        def split_rows(i, _):
            at = pl.ds(pl.multiple_of(i * 32, 32), 32)
            high, low = split(slab_in[b, at, :])
            high_in[b, at, :] = high
            low_in[b, at, :] = low
            return 0

        return lax.fori_loop(0, rows // 32, split_rows, 0)

    lax.fori_loop(0, cols, split_block, 0)

    others(parts, me, lambda src: copy1(src, src).wait_recv())
    for g in range(GROUPS):
        picked = recv1[owner_ref[g] // cols]
        for to in range(cols):
            send2[to, g] = picked[to * CHUNKS:(to + 1) * CHUNKS, :]
    recv2[col] = send2[col]
    others(cols, col, lambda to: copy2(to, col).start())
    others(cols, col, lambda src: copy2(src, src).wait_recv())
    for g in range(GROUPS):
        recv3[col, g] = recv2[owner_ref[g] % cols, g]
    others(cols, col, lambda to: copy3(to, col).start())
    others(cols, col, lambda src: copy3(src, src).wait_recv())

    vec_ref[...] = recv3[...]
    vectors = [recv3[:, g].reshape(half, LANES) for g in range(GROUPS)]
    lane = lax.broadcasted_iota(jnp.int32, (half, LANES), 1)

    def tile_sums(product, lo, hi):
        keep = [
            jnp.where((lane >= BAND * par + lo) & (lane < BAND * par + hi), product, 0.0)
            for par in range(2)
        ]
        return [jnp.sum(k, axis=1, keepdims=True) for k in keep]

    packed = [jnp.zeros((half, LANES), F32) for _ in range(2)]
    for g in range(GROUPS):
        product = vectors[g] * vectors[g]
        for s in range(2):
            sums = tile_sums(product, *segment(g, s))
            packed = [jnp.where(lane == 2 * g + s, sums[par], packed[par]) for par in range(2)]
    for par in range(2):
        square_out[par] = packed[par]

    def square_copy(way, to):
        return pltpu.make_async_remote_copy(
            src_ref=square_out, dst_ref=square_in.at[way], send_sem=st.at[way], recv_sem=rt.at[way],
            device_id={"row": to}, device_id_type=MESH,
        )

    square_copies = [square_copy(0, left), square_copy(1, right)]
    for c in square_copies:
        c.start()

    def partial(b, _):
        high, low = spread(recv3[b])
        depth = high.shape[0]
        first = contract_lanes(jnp.concatenate([high, low], axis=0), high_in[b])
        second = contract_lanes(high, low_in[b])
        total = first[:depth] + (first[depth:] + second)
        raw[:, pl.ds(pl.multiple_of(b * CHUNKS, CHUNKS), CHUNKS), :] = total.reshape(
            depth // CHUNKS, CHUNKS, total.shape[1]
        )
        return 0

    lax.fori_loop(0, cols, partial, 0)

    for n, (g, s, h, t, lo, hi) in enumerate(PAIRS):
        sums = tile_sums(vectors[g] * vectors[h], lo, hi)
        for par in range(2):
            gram[n, par] = jnp.broadcast_to(sums[par], (half, LANES))

    last = me == parts - 1
    first = me == 0

    def of_next(x):
        after = jnp.stack([x[1], pltpu.roll(x[0], half - 1, 0)])
        return jnp.where(last, after, x)

    def of_previous(x):
        before = jnp.stack([pltpu.roll(x[1], 1, 0), x[0]])
        return jnp.where(first, before, x)

    for c in square_copies:
        c.wait()
    mine = jnp.stack(packed)
    after, before = of_next(square_in[0]), of_previous(square_in[1])
    at = lax.broadcasted_iota(jnp.int32, (2, half, 1), 1)
    parity = lax.broadcasted_iota(jnp.int32, (2, half, 1), 0)
    no_next = last & (at == half - 1) & (parity == 1)
    no_previous = first & (at == 0) & (parity == 0)
    for g in range(GROUPS):
        head, tail = slice(2 * g, 2 * g + 1), slice(2 * g + 1, 2 * g + 2)
        own = jnp.where(no_next, 0.0, 2.0 / (mine[:, :, tail] + after[:, :, head] + 1e-06))
        prior = jnp.where(no_previous, 0.0, 2.0 / (before[:, :, tail] + mine[:, :, head] + 1e-06))
        tau[2 * g] = jnp.broadcast_to(prior, (2, half, LANES))
        tau[2 * g + 1] = jnp.broadcast_to(own, (2, half, LANES))

    def exchange(g, n, way):
        to = left if way == 0 else right
        return pltpu.make_async_remote_copy(
            src_ref=send4.at[g, n, way], dst_ref=recv4.at[g, n, way],
            send_sem=s4.at[g, n, way], recv_sem=r4.at[g, n, way],
            device_id={"row": to}, device_id_type=MESH,
        )

    blocks = rows // LANES

    def finish(g, n):
        at = pl.ds(n * LANES, LANES)
        exchange(g, n, 0).wait_recv()
        exchange(g, n, 1).wait_recv()
        head, tail = send4[g, n, 0], send4[g, n, 1]
        prior = tau[2 * g] * (of_previous(recv4[g, n, 1]) + head)
        own = tau[2 * g + 1] * (tail + of_next(recv4[g, n, 0]))
        for par in range(2):
            coef_ref[4 * g + par, :, at] = prior[par]
            coef_ref[4 * g + 2 + par, :, at] = own[par]

    for g in range(GROUPS):
        for n in range(blocks):
            at = pl.ds(n * LANES, LANES)
            if g:
                finish(g - 1, n)
            for s in range(2):
                for par in range(2):
                    x = raw[4 * g + 2 * s + par, :, at]
                    for k, (pg, ps, h, t, _, _) in enumerate(PAIRS):
                        if (pg, ps) == (g, s):
                            x = x - gram[k, par] * coef_ref[4 * h + 2 * t + par, :, at]
                    send4[g, n, s, par] = x
            exchange(g, n, 0).start()
            exchange(g, n, 1).start()
    for n in range(blocks):
        finish(GROUPS - 1, n)

    others(parts, me, lambda to: copy1(to, me).wait_send())
    others(cols, col, lambda to: copy2(to, col).wait_send())
    others(cols, col, lambda to: copy3(to, col).wait_send())
    for g in range(GROUPS):
        for n in range(blocks):
            exchange(g, n, 0).wait_send()
            exchange(g, n, 1).wait_send()


def coefficients(parts, cols, owner, stored, slab):
    rows, length = slab.shape
    half = length // LANES
    vmem, dma = pltpu.VMEM, pltpu.SemaphoreType.DMA
    blocks = rows // LANES
    piece = (cols, GROUPS, CHUNKS, LANES)
    return pl.pallas_call(
        functools.partial(coef_kernel, parts, cols),
        name="coefficients",
        out_shape=(
            jax.ShapeDtypeStruct((4 * GROUPS, half, rows), F32),
            jax.ShapeDtypeStruct(piece, F32),
        ),
        in_specs=[
            pl.BlockSpec(memory_space=pltpu.SMEM),
            pl.BlockSpec(memory_space=pl.ANY),
            pl.BlockSpec(memory_space=pl.ANY),
        ],
        out_specs=(pl.BlockSpec(memory_space=vmem), pl.BlockSpec(memory_space=vmem)),
        scratch_shapes=[
            vmem(stored.shape, F32),
            vmem((cols, rows, WIDE), F32),
            vmem((cols, rows, WIDE), BF16),
            vmem((cols, rows, WIDE), BF16),
            vmem((parts, half, LANES), F32),
            vmem((parts, half, LANES), F32),
            vmem(piece, F32),
            vmem(piece, F32),
            vmem(piece, F32),
            vmem((4 * GROUPS, half, rows), F32),
            vmem((2, half, LANES), F32),
            vmem((2, 2, half, LANES), F32),
            vmem((len(PAIRS), 2, half, LANES), F32),
            vmem((2 * GROUPS, 2, half, LANES), F32),
            vmem((GROUPS, blocks, 2, 2, half, LANES), F32),
            vmem((GROUPS, blocks, 2, 2, half, LANES), F32),
            dma, dma((cols,)),
            dma((parts,)), dma((parts,)),
            dma((cols,)), dma((cols,)),
            dma((cols,)), dma((cols,)),
            dma((2,)), dma((2,)),
            dma((GROUPS, blocks, 2)), dma((GROUPS, blocks, 2)),
        ],
        compiler_params=pltpu.CompilerParams(
            has_side_effects=True, vmem_limit_bytes=40 * 1024 * 1024
        ),
    )(owner, stored, slab)


def update_kernel(coef_ref, vec_ref, slab_ref, out_ref):
    coef = coef_ref[...]
    turned = coef.reshape(coef.shape[0] * coef.shape[1], coef.shape[2]).T
    high, low = split(turned)
    thigh, tlow = spread(vec_ref[0])
    change = jnp.dot(
        jnp.concatenate([high, high], axis=1), jnp.concatenate([tlow, thigh], axis=0),
        preferred_element_type=F32,
    ) + jnp.dot(low, thigh, preferred_element_type=F32)
    out_ref[...] = slab_ref[...] - change


def update(cols, coef, vec, slab):
    rows, length = slab.shape
    return pl.pallas_call(
        update_kernel,
        name="update",
        grid=(cols,),
        out_shape=jax.ShapeDtypeStruct(slab.shape, F32),
        in_specs=[
            pl.BlockSpec((4 * GROUPS, CHUNKS, rows), lambda b: (0, b, 0)),
            pl.BlockSpec((1, GROUPS, CHUNKS, LANES), lambda b: (b, 0, 0, 0)),
            pl.BlockSpec((rows, WIDE), lambda b: (0, b)),
        ],
        out_specs=pl.BlockSpec((rows, WIDE), lambda b: (0, b)),
        compiler_params=pltpu.CompilerParams(vmem_limit_bytes=24 * 1024 * 1024),
    )(coef, vec, slab)


def shards(parts, cols, slab, stored, owner):
    coef, vec = coefficients(parts, cols, owner, stored.reshape(-1, LANES), slab)
    return update(cols, coef, vec, slab)


def solution(mesh):
    placed = (P("col", "row"), P(("row", "col"), None), P())
    body = functools.partial(shards, mesh.shape["row"], mesh.shape["col"])
    return jax.shard_map(
        body, mesh=mesh, in_specs=placed, out_specs=P("col", "row"), check_vma=False
    )
```

time: 664 us -> 71.6 us (0.11); the launches traced: 653 us -> 71.4 us
  waiting for transfers between devices: 240 us -> 0 us
  local copies, waits for them, and re-layouts: 142 us -> 5.08 us
  blocking collectives: 101 us -> 0 us
  matrix products: 77 us -> 0 us
  other arithmetic: 67.1 us -> 0 us
  Pallas kernels: 0 us -> 66.3 us
  between operations: 16.9 us -> 0.01 us
  starting transfers between devices: 8.21 us -> 0 us
    psum x1 -> x0, waiting for transfers between devices: 240 us -> none  [from_root(): return lax.psum(block, axis)]
    all_to_all x1 -> x0, blocking collectives: 101 us -> none  [shards(): lax.all_to_all(gathered, 'row', split_axis=1, concat_axis=0, tiled=True)]
    dot_general x8 -> x0, matrix products: 77 us -> none  [the longest x4 41 us: apply_coef(): jnp.dot(coefs, selector.T, precision=lax.Precision.HIGHEST, preferred_ele...]
    pallas_call x0 -> x2, Pallas kernels: none -> 66.3 us  [the longest x1 59.6 us: coefficients(): pl.pallas_call(functools.partial(coef_kernel, parts, cols), name='coeffic...]
    reshape x24 -> x0, local copies, waits for them, and re-layouts: 53.3 us -> none  [the longest x4 38.1 us: apply_coef(): return values - lane_values.reshape(rows_count, length) * vector_flat[None]]
    sub x1 -> x0, other arithmetic: 39.5 us -> none  [apply_coef(): return values - lane_values.reshape(rows_count, length) * vector_flat[None]]
    transpose x20 -> x0, local copies, waits for them, and re-layouts: 22.6 us -> none  [the longest x4 8.72 us: shards(): head.reshape(owned, parts, tiles_dev).transpose(0, 2, 1)]
    all_to_all x2 -> x0, local copies, waits for them, and re-layouts: 21.3 us -> none  [shards(): lax.all_to_all(slab, 'row', split_axis=0, concat_axis=1, tiled=True)]
  transfers between devices with their start and end apart: 2 -> 0, of which waited for: 1 -> 0; matrix products, arithmetic and copies ran while one was open for 6% -> 0% of each run, Pallas kernels for 0% -> 0%
where the time goes in v1:
time: 71.6 us; the launch traced here: 71.4 us
  Pallas kernels  66.3 us (93%)
  local copies, waits for them, and re-layouts  5.08 us (7%)
    pallas_call x1, Pallas kernels, coefficients(): pl.pallas_call(functools.partial(coef_kernel, parts, cols), name='coeffic...  59.6 us
    pallas_call x1, Pallas kernels, update(): pl.pallas_call(update_kernel, name='update', grid=(cols,), out_shape=jax....  6.72 us
    unnamed x6, local copies, waits for them, and re-layouts  5.08 us

profile of v1, /device:TPU:0, one launch (start us, length us, event | category | flops | bytes accessed | tf_op | source)
XLA Modules:
  0.0 71.4 jit_solution(7766679721922186897)
XLA Ops:
  0.0 0.0 copy-start
  0.0 3.4 %copy-done = f32[256,8192]{1,0:T(8,128)S(1)} copy-done((f32[256,8192]{1,0:T(8,128)S(1)}, f32[256,8192]{1,0:T(8,128)}, u32[]{:S(2)}) %copy-start) | copy-done | bytes 8388632
  3.4 0.0 copy-start.1
  3.4 1.0 %copy-done.1 = f32[1,131072]{1,0:T(1,128)S(1)} copy-done((f32[1,131072]{1,0:T(1,128)S(1)}, f32[1,131072]{1,0:T(1,128)}, u32[]{:S(2)}) %copy-start.1) | copy-done | bytes 524312
  4.4 0.0 copy-start.2
  4.4 0.7 copy-done.2
  5.1 59.6 %coefficients.1 = (f32[16,64,256]{2,1,0:T(8,128)S(1)}, f32[8,4,8,128]{3,2,1,0:T(8,128)S(1)}) custom-call(s32[4]{0:T(128)S(1)} %copy-done.2, f32[1024,128]{1,0:T(8,128)S(1)} %bitcast.1, f32[256,8192]{1,0:T(8,128)S(1)} %copy-done), custom_call_target="tpu_custom_call" | custom-call | tf_op jit(solution)/shard_map/coefficients/pallas_call | solution.py:285
  64.7 6.7 %update.1 = f32[256,8192]{1,0:T(8,128)} custom-call(f32[16,64,256]{2,1,0:T(8,128)S(1)} %get-tuple-element.7.coef_ref, f32[8,4,8,128]{3,2,1,0:T(8,128)S(1)} %get-tuple-element.8.vec_ref, f32[256,8192]{1,0:T(8,128)S(1)} %copy-done), custom_call_target="tpu_custom_call" | custom-call | tf_op jit(solution)/shard_map/update/pallas_call | solution.py:342
Async XLA Ops:
  0.0 3.4 %copy-start = (f32[256,8192]{1,0:T(8,128)S(1)}, f32[256,8192]{1,0:T(8,128)}, u32[]{:S(2)}) copy-start(f32[256,8192]{1,0:T(8,128)} %slab_ref.3) | copy-start | bytes 25165828
  3.4 1.0 %copy-start.1 = (f32[1,131072]{1,0:T(1,128)S(1)}, f32[1,131072]{1,0:T(1,128)}, u32[]{:S(2)}) copy-start(f32[1,131072]{1,0:T(1,128)} %param.4) | copy-start | bytes 1572868
  4.4 0.7 copy-start.2

commit v2 on v1

v2 whole, which is shorter than its diff:
```python
import functools

import jax
import jax.numpy as jnp
from jax import lax
from jax.experimental import pallas as pl
from jax.experimental.pallas import tpu as pltpu
from jax.sharding import PartitionSpec as P

BAND = 64
GROUPS = 4
LANES = 128
CHUNKS = 8
WIDE = CHUNKS * LANES
MESH = pl.DeviceIdType.MESH
F32 = jnp.float32
BF16 = jnp.bfloat16


def offset_of(group):
    return 1 + (37 * group + 11) % 63


def segment(group, side):
    return (0, offset_of(group)) if side == 0 else (offset_of(group), BAND)


PAIRS = []
for _g in range(GROUPS):
    for _s in range(2):
        for _h in range(_g):
            for _t in range(2):
                _lo = max(segment(_g, _s)[0], segment(_h, _t)[0])
                _hi = min(segment(_g, _s)[1], segment(_h, _t)[1])
                if _lo < _hi:
                    PAIRS.append((_g, _s, _h, _t, _lo, _hi))


def split(x):
    high = x.astype(BF16)
    return high, (x - high.astype(F32)).astype(BF16)


def spread(vectors):
    lane = lax.broadcasted_iota(jnp.int32, (CHUNKS, WIDE), 1)
    row = lax.broadcasted_iota(jnp.int32, (CHUNKS, WIDE), 0)
    here = (lane // LANES) == row
    within = lane % LANES
    zero = jnp.zeros((CHUNKS, WIDE), F32)
    highs, lows = [], []
    for g in range(GROUPS):
        v = vectors[g]
        high = v.astype(BF16).astype(F32)
        wide_high = jnp.concatenate([high] * CHUNKS, axis=1)
        wide_low = jnp.concatenate([v - high] * CHUNKS, axis=1)
        for s in range(2):
            lo, hi = segment(g, s)
            masks = [
                here & (within >= BAND * par + lo) & (within < BAND * par + hi) for par in range(2)
            ]
            for wide, into in ((wide_high, highs), (wide_low, lows)):
                both = jnp.concatenate([jnp.where(m, wide, zero) for m in masks], axis=0)
                into.append(both.astype(BF16))
    return jnp.concatenate(highs, axis=0), jnp.concatenate(lows, axis=0)


def contract_lanes(a, b):
    return lax.dot_general(a, b, (((1,), (1,)), ((), ())), preferred_element_type=F32)


def coef_kernel(
    parts, cols, owner_hbm, row_in, slab_ref, coef_ref, vec_ref, slab_in,
    owner_ref, high_in, low_in, send1, recv1, recv3,
    raw, packed, square_out, square_in, gram, tau, send4, recv4,
    owner_sem, slab_sem, s1, r1, s3, r3, st, rt, s4, r4,
):
    half = cols * CHUNKS
    me = lax.axis_index("row")
    col = lax.axis_index("col")
    left = lax.rem(me + parts - 1, parts)
    right = lax.rem(me + 1, parts)

    def others(size, mine, step):
        def body(r, _):
            step(lax.rem(mine + r, size))
            return 0

        lax.fori_loop(1, size, body, 0)

    barrier = pltpu.get_barrier_semaphore()
    devices = parts * cols
    mine = me * cols + col
    others(devices, mine, lambda to: pl.semaphore_signal(
        barrier, inc=1, device_id={"row": to // cols, "col": lax.rem(to, cols)}, device_id_type=MESH))
    owner_copy = pltpu.make_async_copy(owner_hbm, owner_ref, owner_sem)
    owner_copy.start()

    def slab_copy(b):
        return pltpu.make_async_copy(
            slab_ref.at[:, pl.ds(pl.multiple_of(b * WIDE, WIDE), WIDE)], slab_in.at[b], slab_sem.at[b]
        )

    lax.fori_loop(0, cols, lambda b, _: (slab_copy(b).start(), 0)[1], 0)

    low_lanes = lax.broadcasted_iota(jnp.int32, (half, LANES), 1) < BAND
    for q in range(parts // 2):
        even = row_in[pl.ds(q, half, stride=parts), :]
        odd = row_in[pl.ds(q + parts // 2, half, stride=parts), :]
        first_half = jnp.where(low_lanes, even, pltpu.roll(odd, BAND, 1))
        second_half = jnp.where(low_lanes, pltpu.roll(even, BAND, 1), odd)
        send1[pl.ds(2 * q * cols, cols)] = first_half.reshape(cols, CHUNKS, LANES)
        send1[pl.ds((2 * q + 1) * cols, cols)] = second_half.reshape(cols, CHUNKS, LANES)
    recv1[mine] = send1[mine]

    def copy1(to):
        return pltpu.make_async_remote_copy(
            src_ref=send1.at[to], dst_ref=recv1.at[mine], send_sem=s1, recv_sem=r1,
            device_id={"row": to // cols, "col": lax.rem(to, cols)}, device_id_type=MESH,
        )

    def copy3(to, source):
        return pltpu.make_async_remote_copy(
            src_ref=recv3.at[source], dst_ref=recv3.at[source], send_sem=s3.at[to], recv_sem=r3.at[source],
            device_id={"col": to}, device_id_type=MESH,
        )

    pl.semaphore_wait(barrier, devices - 1)
    others(devices, mine, lambda to: copy1(to).start())

    rows = slab_in.shape[1]

    def split_block(b, _):
        slab_copy(b).wait()

        def split_rows(i, _):
            at = pl.ds(pl.multiple_of(i * 32, 32), 32)
            high, low = split(slab_in[b, at, :])
            high_in[b, at, :] = high
            low_in[b, at, :] = low
            return 0

        return lax.fori_loop(0, rows // 32, split_rows, 0)

    lax.fori_loop(0, cols, split_block, 0)

    owner_copy.wait()
    every = recv1.at[pl.ds(0, devices - 1)]
    pltpu.make_async_copy(every, every, r1).wait()
    for g in range(GROUPS):
        recv3[col, g] = recv1[owner_ref[g]]
    others(cols, col, lambda to: copy3(to, col).start())

    lane8 = lax.broadcasted_iota(jnp.int32, (CHUNKS, LANES), 1)

    def piece_sums(product, lane, lo, hi):
        return [
            jnp.sum(
                jnp.where((lane >= BAND * par + lo) & (lane < BAND * par + hi), product, 0.0),
                axis=1, keepdims=True,
            )
            for par in range(2)
        ]

    def partial(b):
        at = pl.ds(pl.multiple_of(b * CHUNKS, CHUNKS), CHUNKS)
        piece = recv3[b]
        high, low = spread(piece)
        depth = high.shape[0]
        one = contract_lanes(jnp.concatenate([high, low], axis=0), high_in[b])
        two = contract_lanes(high, low_in[b])
        total = one[:depth] + (one[depth:] + two)
        raw[:, at, :] = total.reshape(depth // CHUNKS, CHUNKS, total.shape[1])
        squares = [jnp.zeros((CHUNKS, LANES), F32) for _ in range(2)]
        for g in range(GROUPS):
            for s in range(2):
                sums = piece_sums(piece[g] * piece[g], lane8, *segment(g, s))
                squares = [jnp.where(lane8 == 2 * g + s, sums[par], squares[par]) for par in range(2)]
        for par in range(2):
            packed[par, at, :] = squares[par]

    def partial_of(src):
        copy3(src, src).wait_recv()
        partial(src)

    partial(col)
    others(cols, col, partial_of)

    vec_ref[...] = recv3[...]
    vectors = [recv3[:, g].reshape(half, LANES) for g in range(GROUPS)]
    lane = lax.broadcasted_iota(jnp.int32, (half, LANES), 1)

    square_out[...] = jnp.concatenate([packed[0], packed[1]], axis=0).T[:2 * GROUPS, :]

    def square_copy(way, to):
        return pltpu.make_async_remote_copy(
            src_ref=square_out, dst_ref=square_in.at[way], send_sem=st.at[way], recv_sem=rt.at[way],
            device_id={"row": to}, device_id_type=MESH,
        )

    square_copies = [square_copy(0, left), square_copy(1, right)]
    for c in square_copies:
        c.start()

    blocks = rows // LANES
    steps = [(n, par) for n in range(blocks) for par in range(2)]
    last = me == parts - 1
    first = me == 0

    def exchange(g, n, way, par):
        to = left if way == 0 else right
        return pltpu.make_async_remote_copy(
            src_ref=send4.at[g, n, way, par], dst_ref=recv4.at[g, n, way, par],
            send_sem=s4.at[g, n, way, par], recv_sem=r4.at[g, n, way, par],
            device_id={"row": to}, device_id_type=MESH,
        )

    def prepare(g, n, par):
        at = pl.ds(n * LANES, LANES)
        for s in range(2):
            x = raw[4 * g + 2 * s + par, :, at]
            for k, (pg, ps, h, t, _, _) in enumerate(PAIRS):
                if (pg, ps) == (g, s):
                    x = x - gram[k, par] * coef_ref[4 * h + 2 * t + par, :, at]
            send4[g, n, s, par] = x
        exchange(g, n, 0, par).start()
        exchange(g, n, 1, par).start()

    def of_next(x, par):
        return jnp.where(last, pltpu.roll(x, half - 1, 0), x) if par else x

    def of_previous(x, par):
        return x if par else jnp.where(first, pltpu.roll(x, 1, 0), x)

    def next_parity(par):
        return jnp.where(last, 1 - par, par)

    def previous_parity(par):
        return jnp.where(first, 1 - par, par)

    def finish(g, n, par):
        at = pl.ds(n * LANES, LANES)
        after, before = next_parity(par), previous_parity(par)
        exchange(g, n, 0, after).wait_recv()
        exchange(g, n, 1, before).wait_recv()
        head, tail = send4[g, n, 0, par], send4[g, n, 1, par]
        coef_ref[4 * g + par, :, at] = tau[2 * g, par] * (of_previous(recv4[g, n, 1, before], par) + head)
        coef_ref[4 * g + 2 + par, :, at] = tau[2 * g + 1, par] * (tail + of_next(recv4[g, n, 0, after], par))

    for n, par in steps:
        prepare(0, n, par)

    for k, (g, s, h, t, lo, hi) in enumerate(PAIRS):
        sums = piece_sums(vectors[g] * vectors[h], lane, lo, hi)
        for par in range(2):
            gram[k, par] = jnp.broadcast_to(sums[par], (half, LANES))

    for c in square_copies:
        c.wait()

    def turned(way):
        full = jnp.concatenate([square_in[way]] * (2 * half // (2 * GROUPS)), axis=0).T
        return [full[:half], full[half:]]

    right_squares, left_squares = turned(0), turned(1)
    at = lax.broadcasted_iota(jnp.int32, (half, 1), 0)
    for par in range(2):
        after = of_next(jnp.where(last, right_squares[1 - par], right_squares[par]), par)
        before = of_previous(jnp.where(first, left_squares[1 - par], left_squares[par]), par)
        here = packed[par]
        for g in range(GROUPS):
            head, tail = slice(2 * g, 2 * g + 1), slice(2 * g + 1, 2 * g + 2)
            own = 2.0 / (here[:, tail] + after[:, head] + 1e-06)
            prior = 2.0 / (before[:, tail] + here[:, head] + 1e-06)
            if par:
                own = jnp.where(last & (at == half - 1), 0.0, own)
            else:
                prior = jnp.where(first & (at == 0), 0.0, prior)
            tau[2 * g, par] = jnp.broadcast_to(prior, (half, LANES))
            tau[2 * g + 1, par] = jnp.broadcast_to(own, (half, LANES))

    for g in range(GROUPS):
        for n, par in steps:
            finish(g, n, par)
            if g + 1 < GROUPS:
                prepare(g + 1, n, par)

    sent = send1.at[pl.ds(0, devices - 1)]
    pltpu.make_async_copy(sent, sent, s1).wait()
    others(cols, col, lambda to: copy3(to, col).wait_send())
    for g in range(GROUPS):
        for n, par in steps:
            exchange(g, n, 0, par).wait_send()
            exchange(g, n, 1, par).wait_send()


def coefficients(parts, cols, owner, stored, slab):
    rows, length = slab.shape
    half = length // LANES
    vmem, dma = pltpu.VMEM, pltpu.SemaphoreType.DMA
    blocks = rows // LANES
    piece = (cols, GROUPS, CHUNKS, LANES)
    return pl.pallas_call(
        functools.partial(coef_kernel, parts, cols),
        name="coefficients",
        out_shape=(
            jax.ShapeDtypeStruct((4 * GROUPS, half, rows), F32),
            jax.ShapeDtypeStruct(piece, F32),
            jax.ShapeDtypeStruct((cols, rows, WIDE), F32),
        ),
        in_specs=[
            pl.BlockSpec(memory_space=pltpu.HBM),
            pl.BlockSpec(memory_space=vmem),
            pl.BlockSpec(memory_space=pltpu.HBM),
        ],
        out_specs=(pl.BlockSpec(memory_space=vmem),) * 3,
        scratch_shapes=[
            pltpu.SMEM((GROUPS,), jnp.int32),
            vmem((cols, rows, WIDE), BF16),
            vmem((cols, rows, WIDE), BF16),
            vmem((parts * cols, CHUNKS, LANES), F32),
            vmem((parts * cols, CHUNKS, LANES), F32),
            vmem(piece, F32),
            vmem((4 * GROUPS, half, rows), F32),
            vmem((2, half, LANES), F32),
            vmem((2 * GROUPS, 2 * half), F32),
            vmem((2, 2 * GROUPS, 2 * half), F32),
            vmem((len(PAIRS), 2, half, LANES), F32),
            vmem((2 * GROUPS, 2, half, LANES), F32),
            vmem((GROUPS, blocks, 2, 2, half, LANES), F32),
            vmem((GROUPS, blocks, 2, 2, half, LANES), F32),
            dma, dma((cols,)),
            dma, dma,
            dma((cols,)), dma((cols,)),
            dma((2,)), dma((2,)),
            dma((GROUPS, blocks, 2, 2)), dma((GROUPS, blocks, 2, 2)),
        ],
        compiler_params=pltpu.CompilerParams(
            has_side_effects=True, collective_id=0, vmem_limit_bytes=40 * 1024 * 1024
        ),
    )(owner, stored, slab)


def update_kernel(cols, coef_ref, vec_ref, slab_ref, out_ref, ready, sem):
    slots = ready.shape[0]

    def copy(b):
        slot = lax.rem(b, slots)
        at = pl.ds(pl.multiple_of(b * WIDE, WIDE), WIDE)
        return pltpu.make_async_copy(ready.at[slot], out_ref.at[:, at], sem.at[slot])

    def block(b, _):
        @pl.when(b >= slots)
        def _():
            copy(b - slots).wait()

        coef = coef_ref[:, pl.ds(pl.multiple_of(b * CHUNKS, CHUNKS), CHUNKS), :]
        turned = coef.reshape(coef.shape[0] * coef.shape[1], coef.shape[2]).T
        high, low = split(turned)
        thigh, tlow = spread(vec_ref[b])
        change = jnp.dot(
            jnp.concatenate([high, high], axis=1), jnp.concatenate([tlow, thigh], axis=0),
            preferred_element_type=F32,
        ) + jnp.dot(low, thigh, preferred_element_type=F32)
        ready[lax.rem(b, slots)] = slab_ref[b] - change
        copy(b).start()
        return 0

    lax.fori_loop(0, cols, block, 0)
    lax.fori_loop(max(cols - slots, 0), cols, lambda b, _: (copy(b).wait(), 0)[1], 0)


def update(cols, coef, vec, slab_in):
    blocks, rows, wide = slab_in.shape
    return pl.pallas_call(
        functools.partial(update_kernel, cols),
        name="update",
        out_shape=jax.ShapeDtypeStruct((rows, blocks * wide), F32),
        in_specs=[pl.BlockSpec(memory_space=pltpu.VMEM)] * 3,
        out_specs=pl.BlockSpec(memory_space=pltpu.HBM),
        scratch_shapes=[pltpu.VMEM((3, rows, wide), F32), pltpu.SemaphoreType.DMA((3,))],
        compiler_params=pltpu.CompilerParams(vmem_limit_bytes=24 * 1024 * 1024),
    )(coef, vec, slab_in)


def shards(parts, cols, slab, stored, owner):
    coef, vec, slab_in = coefficients(parts, cols, owner, stored.reshape(-1, LANES), slab)
    return update(cols, coef, vec, slab_in)


def solution(mesh):
    placed = (P("col", "row"), P(("row", "col"), None), P())
    body = functools.partial(shards, mesh.shape["row"], mesh.shape["col"])
    return jax.shard_map(
        body, mesh=mesh, in_specs=placed, out_specs=P("col", "row"), check_vma=False
    )
```

time: 71.6 us -> 55.2 us (0.77)
  Pallas kernels: 66.3 us -> 53.3 us
  local copies, waits for them, and re-layouts: 5.08 us -> 1.7 us
    pallas_call x1, Pallas kernels: 59.6 us -> 48.4 us  [coefficients(): pl.pallas_call(functools.partial(coef_kernel, parts, cols), name='coeffic...]
    unnamed x6 -> x4, local copies, waits for them, and re-layouts: 5.08 us -> 1.7 us
    pallas_call x1, Pallas kernels: 6.72 us -> 4.9 us  [update(): pl.pallas_call(functools.partial(update_kernel, cols), name='update', out...]
where the time goes in v2:
time: 55.2 us; the launch traced here: 55 us
  Pallas kernels  53.3 us (97%)
  local copies, waits for them, and re-layouts  1.7 us (3%)
    pallas_call x1, Pallas kernels, coefficients(): pl.pallas_call(functools.partial(coef_kernel, parts, cols), name='coeffic...  48.4 us
    pallas_call x1, Pallas kernels, update(): pl.pallas_call(functools.partial(update_kernel, cols), name='update', out...  4.9 us
    unnamed x4, local copies, waits for them, and re-layouts  1.7 us

profile of v2, /device:TPU:0, one launch (start us, length us, event | category | flops | bytes accessed | tf_op | source)
XLA Modules:
  0.0 55.0 jit_solution(15517053958751239659)
XLA Ops:
  0.0 0.0 copy-start
  0.0 1.0 %copy-done = f32[1,131072]{1,0:T(1,128)S(1)} copy-done((f32[1,131072]{1,0:T(1,128)S(1)}, f32[1,131072]{1,0:T(1,128)}, u32[]{:S(2)}) %copy-start) | copy-done | bytes 524312
  1.0 0.0 copy-start.1
  1.0 0.7 %copy-done.1 = s32[4]{0:T(128)S(1)} copy-done((s32[4]{0:T(128)S(1)}, s32[4]{0:T(128)}, u32[]{:S(2)}) %copy-start.1) | copy-done | bytes 40
  1.7 48.4 %coefficients.1 = (f32[16,64,256]{2,1,0:T(8,128)S(1)}, f32[8,4,8,128]{3,2,1,0:T(8,128)S(1)}, f32[8,256,1024]{2,1,0:T(8,128)S(1)}) custom-call(s32[4]{0:T(128)S(1)} %copy-done.1, f32[1024,128]{1,0:T(8,128)S(1)} %bitcast.1, f32[256,8192]{1,0:T(8,128)} %slab_ref.1), custom_call_target="tpu_custom_call" | custom-call | tf_op jit(solution)/shard_map/coefficients/pallas_call | solution.py:302
  50.1 4.9 %update.1 = f32[256,8192]{1,0:T(8,128)} custom-call(f32[16,64,256]{2,1,0:T(8,128)S(1)} %get-tuple-element.8.coef_ref, f32[8,4,8,128]{3,2,1,0:T(8,128)S(1)} %get-tuple-element.9.vec_ref, f32[8,256,1024]{2,1,0:T(8,128)S(1)} %get-tuple-element.10.slab_ref), custom_call_target="tpu_custom_call" | custom-call | tf_op jit(solution)/shard_map/update/pallas_call | solution.py:374
Async XLA Ops:
  0.0 1.0 %copy-start = (f32[1,131072]{1,0:T(1,128)S(1)}, f32[1,131072]{1,0:T(1,128)}, u32[]{:S(2)}) copy-start(f32[1,131072]{1,0:T(1,128)} %param.4) | copy-start | bytes 1572868
  1.0 0.7 %copy-start.1 = (s32[4]{0:T(128)S(1)}, s32[4]{0:T(128)}, u32[]{:S(2)}) copy-start(s32[4]{0:T(128)} %owner_hbm.1) | copy-start | bytes 52

commit v3 on v2

--- a/solution.py
+++ b/solution.py
@@ -12,6 +12,7 @@
 LANES = 128
 CHUNKS = 8
 WIDE = CHUNKS * LANES
+PIECES = 2
 MESH = pl.DeviceIdType.MESH
 F32 = jnp.float32
 BF16 = jnp.bfloat16
@@ -69,10 +70,10 @@
 
 
 def coef_kernel(
-    parts, cols, owner_hbm, row_in, slab_ref, coef_ref, vec_ref, slab_in,
-    owner_ref, high_in, low_in, send1, recv1, recv3,
+    parts, cols, owner_hbm, stored_ref, slab_ref, coef_ref, vec_ref, slab_in,
+    owner_ref, row_in, high_in, low_in, send1, recv1, recv3,
     raw, packed, square_out, square_in, gram, tau, send4, recv4,
-    owner_sem, slab_sem, s1, r1, s3, r3, st, rt, s4, r4,
+    owner_sem, row_sem, slab_sem, s1, r1, s3, r3, st, rt, s4, r4,
 ):
     half = cols * CHUNKS
     me = lax.axis_index("row")
@@ -94,6 +95,8 @@
         barrier, inc=1, device_id={"row": to // cols, "col": lax.rem(to, cols)}, device_id_type=MESH))
     owner_copy = pltpu.make_async_copy(owner_hbm, owner_ref, owner_sem)
     owner_copy.start()
+    row_copy = pltpu.make_async_copy(stored_ref, row_in, row_sem)
+    row_copy.start()
 
     def slab_copy(b):
         return pltpu.make_async_copy(
@@ -102,6 +105,7 @@
 
     lax.fori_loop(0, cols, lambda b, _: (slab_copy(b).start(), 0)[1], 0)
 
+    row_copy.wait()
     low_lanes = lax.broadcasted_iota(jnp.int32, (half, LANES), 1) < BAND
     for q in range(parts // 2):
         even = row_in[pl.ds(q, half, stride=parts), :]
@@ -178,12 +182,20 @@
         for par in range(2):
             packed[par, at, :] = squares[par]
 
-    def partial_of(src):
+    pair = (col // 2) * 2
+    copy3(lax.rem(col, 2) * -2 + 1 + col, lax.rem(col, 2) * -2 + 1 + col).wait_recv()
+    partial(pair)
+    partial(pair + 1)
+
+    def partial_pair(i, _):
+        src = lax.rem(pair + 2 * i, cols)
         copy3(src, src).wait_recv()
+        copy3(src + 1, src + 1).wait_recv()
         partial(src)
-
-    partial(col)
-    others(cols, col, partial_of)
+        partial(src + 1)
+        return 0
+
+    lax.fori_loop(1, cols // 2, partial_pair, 0)
 
     vec_ref[...] = recv3[...]
     vectors = [recv3[:, g].reshape(half, LANES) for g in range(GROUPS)]
@@ -202,28 +214,31 @@
         c.start()
 
     blocks = rows // LANES
-    steps = [(n, par) for n in range(blocks) for par in range(2)]
+    part = half // PIECES
+    steps = [(n, q, par) for n in range(blocks) for q in range(PIECES) for par in range(2)]
     last = me == parts - 1
     first = me == 0
 
-    def exchange(g, n, way, par):
+    def exchange(g, n, way, par, q):
         to = left if way == 0 else right
+        at = pl.ds(q * part, part)
         return pltpu.make_async_remote_copy(
-            src_ref=send4.at[g, n, way, par], dst_ref=recv4.at[g, n, way, par],
-            send_sem=s4.at[g, n, way, par], recv_sem=r4.at[g, n, way, par],
+            src_ref=send4.at[g, n, way, par, at], dst_ref=recv4.at[g, n, way, par, at],
+            send_sem=s4.at[g, n, way, par, q], recv_sem=r4.at[g, n, way, par, q],
             device_id={"row": to}, device_id_type=MESH,
         )
 
-    def prepare(g, n, par):
+    def prepare(g, n, q, par):
         at = pl.ds(n * LANES, LANES)
+        tiles = pl.ds(q * part, part)
         for s in range(2):
-            x = raw[4 * g + 2 * s + par, :, at]
+            x = raw[4 * g + 2 * s + par, tiles, at]
             for k, (pg, ps, h, t, _, _) in enumerate(PAIRS):
                 if (pg, ps) == (g, s):
-                    x = x - gram[k, par] * coef_ref[4 * h + 2 * t + par, :, at]
-            send4[g, n, s, par] = x
-        exchange(g, n, 0, par).start()
-        exchange(g, n, 1, par).start()
+                    x = x - gram[k, par, tiles] * coef_ref[4 * h + 2 * t + par, tiles, at]
+            send4[g, n, s, par, tiles] = x
+        exchange(g, n, 0, par, q).start()
+        exchange(g, n, 1, par, q).start()
 
     def of_next(x, par):
         return jnp.where(last, pltpu.roll(x, half - 1, 0), x) if par else x
@@ -237,17 +252,54 @@
     def previous_parity(par):
         return jnp.where(first, 1 - par, par)
 
-    def finish(g, n, par):
+    def heads_after(g, n, q, par):
+        from_ref = recv4.at[g, n, 0, next_parity(par)]
+        if par == 0:
+            exchange(g, n, 0, next_parity(par), q).wait_recv()
+            return from_ref[q * part:(q + 1) * part]
+
+        @pl.when(jnp.logical_not(last))
+        def _():
+            exchange(g, n, 0, 1, q).wait_recv()
+
+        @pl.when(last)
+        def _():
+            if q == 0:
+                exchange(g, n, 0, 0, 0).wait_recv()
+            if q + 1 < PIECES:
+                exchange(g, n, 0, 0, q + 1).wait_recv()
+
+        def shifted():
+            if q + 1 < PIECES:
+                return from_ref[q * part + 1:(q + 1) * part + 1]
+            return pltpu.roll(from_ref[q * part:(q + 1) * part], part - 1, 0)
+
+        return lax.cond(last, shifted, lambda: from_ref[q * part:(q + 1) * part])
+
+    def tails_before(g, n, q, par):
+        from_ref = recv4.at[g, n, 1, previous_parity(par)]
+        exchange(g, n, 1, previous_parity(par), q).wait_recv()
+        if par:
+            return from_ref[q * part:(q + 1) * part]
+
+        def shifted():
+            if q:
+                return from_ref[q * part - 1:(q + 1) * part - 1]
+            return pltpu.roll(from_ref[0:part], 1, 0)
+
+        return lax.cond(first, shifted, lambda: from_ref[q * part:(q + 1) * part])
+
+    def finish(g, n, q, par):
         at = pl.ds(n * LANES, LANES)
-        after, before = next_parity(par), previous_parity(par)
-        exchange(g, n, 0, after).wait_recv()
-        exchange(g, n, 1, before).wait_recv()
-        head, tail = send4[g, n, 0, par], send4[g, n, 1, par]
-        coef_ref[4 * g + par, :, at] = tau[2 * g, par] * (of_previous(recv4[g, n, 1, before], par) + head)
-        coef_ref[4 * g + 2 + par, :, at] = tau[2 * g + 1, par] * (tail + of_next(recv4[g, n, 0, after], par))
-
-    for n, par in steps:
-        prepare(0, n, par)
+        tiles = pl.ds(q * part, part)
+        after = heads_after(g, n, q, par)
+        before = tails_before(g, n, q, par)
+        head, tail = send4[g, n, 0, par, tiles], send4[g, n, 1, par, tiles]
+        coef_ref[4 * g + par, tiles, at] = tau[2 * g, par, tiles] * (before + head)
+        coef_ref[4 * g + 2 + par, tiles, at] = tau[2 * g + 1, par, tiles] * (tail + after)
+
+    for n, q, par in steps:
+        prepare(0, n, q, par)
 
     for k, (g, s, h, t, lo, hi) in enumerate(PAIRS):
         sums = piece_sums(vectors[g] * vectors[h], lane, lo, hi)
@@ -279,18 +331,18 @@
             tau[2 * g + 1, par] = jnp.broadcast_to(own, (half, LANES))
 
     for g in range(GROUPS):
-        for n, par in steps:
-            finish(g, n, par)
+        for n, q, par in steps:
+            finish(g, n, q, par)
             if g + 1 < GROUPS:
-                prepare(g + 1, n, par)
+                prepare(g + 1, n, q, par)
 
     sent = send1.at[pl.ds(0, devices - 1)]
     pltpu.make_async_copy(sent, sent, s1).wait()
     others(cols, col, lambda to: copy3(to, col).wait_send())
     for g in range(GROUPS):
-        for n, par in steps:
-            exchange(g, n, 0, par).wait_send()
-            exchange(g, n, 1, par).wait_send()
+        for n, q, par in steps:
+            exchange(g, n, 0, par, q).wait_send()
+            exchange(g, n, 1, par, q).wait_send()
 
 
 def coefficients(parts, cols, owner, stored, slab):
@@ -309,12 +361,13 @@
         ),
         in_specs=[
             pl.BlockSpec(memory_space=pltpu.HBM),
-            pl.BlockSpec(memory_space=vmem),
+            pl.BlockSpec(memory_space=pltpu.HBM),
             pl.BlockSpec(memory_space=pltpu.HBM),
         ],
         out_specs=(pl.BlockSpec(memory_space=vmem),) * 3,
         scratch_shapes=[
             pltpu.SMEM((GROUPS,), jnp.int32),
+            vmem(stored.shape, F32),
             vmem((cols, rows, WIDE), BF16),
             vmem((cols, rows, WIDE), BF16),
             vmem((parts * cols, CHUNKS, LANES), F32),
@@ -328,16 +381,16 @@
             vmem((2 * GROUPS, 2, half, LANES), F32),
             vmem((GROUPS, blocks, 2, 2, half, LANES), F32),
             vmem((GROUPS, blocks, 2, 2, half, LANES), F32),
-            dma, dma((cols,)),
+            dma, dma, dma((cols,)),
             dma, dma,
             dma((cols,)), dma((cols,)),
             dma((2,)), dma((2,)),
-            dma((GROUPS, blocks, 2, 2)), dma((GROUPS, blocks, 2, 2)),
+            dma((GROUPS, blocks, 2, 2, PIECES)), dma((GROUPS, blocks, 2, 2, PIECES)),
         ],
         compiler_params=pltpu.CompilerParams(
             has_side_effects=True, collective_id=0, vmem_limit_bytes=40 * 1024 * 1024
         ),
-    )(owner, stored, slab)
+    )(*(pltpu.with_memory_space_constraint(x, pltpu.HBM) for x in (owner, stored, slab)))
 
 
 def update_kernel(cols, coef_ref, vec_ref, slab_ref, out_ref, ready, sem):
@@ -348,11 +401,7 @@
         at = pl.ds(pl.multiple_of(b * WIDE, WIDE), WIDE)
         return pltpu.make_async_copy(ready.at[slot], out_ref.at[:, at], sem.at[slot])
 
-    def block(b, _):
-        @pl.when(b >= slots)
-        def _():
-            copy(b - slots).wait()
-
+    def block(b):
         coef = coef_ref[:, pl.ds(pl.multiple_of(b * CHUNKS, CHUNKS), CHUNKS), :]
         turned = coef.reshape(coef.shape[0] * coef.shape[1], coef.shape[2]).T
         high, low = split(turned)
@@ -362,10 +411,20 @@
             preferred_element_type=F32,
         ) + jnp.dot(low, thigh, preferred_element_type=F32)
         ready[lax.rem(b, slots)] = slab_ref[b] - change
-        copy(b).start()
+
+    def two(i, _):
+        @pl.when(i >= slots // 2)
+        def _():
+            copy(2 * i - slots).wait()
+            copy(2 * i + 1 - slots).wait()
+
+        block(2 * i)
+        block(2 * i + 1)
+        copy(2 * i).start()
+        copy(2 * i + 1).start()
         return 0
 
-    lax.fori_loop(0, cols, block, 0)
+    lax.fori_loop(0, cols // 2, two, 0)
     lax.fori_loop(max(cols - slots, 0), cols, lambda b, _: (copy(b).wait(), 0)[1], 0)
 
 
@@ -377,7 +436,7 @@
         out_shape=jax.ShapeDtypeStruct((rows, blocks * wide), F32),
         in_specs=[pl.BlockSpec(memory_space=pltpu.VMEM)] * 3,
         out_specs=pl.BlockSpec(memory_space=pltpu.HBM),
-        scratch_shapes=[pltpu.VMEM((3, rows, wide), F32), pltpu.SemaphoreType.DMA((3,))],
+        scratch_shapes=[pltpu.VMEM((4, rows, wide), F32), pltpu.SemaphoreType.DMA((4,))],
         compiler_params=pltpu.CompilerParams(vmem_limit_bytes=24 * 1024 * 1024),
     )(coef, vec, slab_in)
 

time: 55.2 us -> 51.8 us (0.938)
  local copies, waits for them, and re-layouts: 1.7 us -> 0 us
  Pallas kernels: 53.3 us -> 51.6 us
    pallas_call x1, Pallas kernels: 48.4 us -> 46.7 us  [coefficients(): pl.pallas_call(functools.partial(coef_kernel, parts, cols), name='coeffic...]
    unnamed x4 -> x0, local copies, waits for them, and re-layouts: 1.7 us -> none
where the time goes in v3:
time: 51.8 us; the launch traced here: 51.7 us
  Pallas kernels  51.6 us (100%)
    pallas_call x1, Pallas kernels, coefficients(): pl.pallas_call(functools.partial(coef_kernel, parts, cols), name='coeffic...  46.7 us
    pallas_call x1, Pallas kernels, update(): pl.pallas_call(functools.partial(update_kernel, cols), name='update', out...  4.92 us

profile of v3, /device:TPU:0, one launch (start us, length us, event | category | flops | bytes accessed | tf_op | source)
XLA Modules:
  0.0 51.7 jit_solution(8831407775803427801)
XLA Ops:
  0.0 46.7 %coefficients.1 = (f32[16,64,256]{2,1,0:T(8,128)S(1)}, f32[8,4,8,128]{3,2,1,0:T(8,128)S(1)}, f32[8,256,1024]{2,1,0:T(8,128)S(1)}) custom-call(s32[4]{0:T(128)} %owner_hbm.1, f32[1024,128]{1,0:T(8,128)} %bitcast.1, f32[256,8192]{1,0:T(8,128)} %slab_ref.1), custom_call_target="tpu_custom_call" | custom-call | tf_op jit(solution)/shard_map/coefficients/pallas_call | solution.py:354
  46.7 4.9 %update.1 = f32[256,8192]{1,0:T(8,128)} custom-call(f32[16,64,256]{2,1,0:T(8,128)S(1)} %get-tuple-element.8.coef_ref, f32[8,4,8,128]{3,2,1,0:T(8,128)S(1)} %get-tuple-element.9.vec_ref, f32[8,256,1024]{2,1,0:T(8,128)S(1)} %get-tuple-element.10.slab_ref), custom_call_target="tpu_custom_call" | custom-call | tf_op jit(solution)/shard_map/update/pallas_call | solution.py:433

commit v4 on v3

--- a/solution.py
+++ b/solution.py
@@ -71,9 +71,9 @@
 
 def coef_kernel(
     parts, cols, owner_hbm, stored_ref, slab_ref, coef_ref, vec_ref, slab_in,
-    owner_ref, row_in, high_in, low_in, send1, recv1, recv3,
+    owner_ref, row_in, high_in, low_in, send_a, recv_a, send_b, recv_b, pick_a, from_a, pick_b, from_b, recv3,
     raw, packed, square_out, square_in, gram, tau, send4, recv4,
-    owner_sem, row_sem, slab_sem, s1, r1, s3, r3, st, rt, s4, r4,
+    owner_sem, row_sem, slab_sem, sa, ra, sb, rb, spa, rpa, spb, rpb, s3, r3, st, rt, s4, r4,
 ):
     half = cols * CHUNKS
     me = lax.axis_index("row")
@@ -89,10 +89,10 @@
         lax.fori_loop(1, size, body, 0)
 
     barrier = pltpu.get_barrier_semaphore()
-    devices = parts * cols
-    mine = me * cols + col
-    others(devices, mine, lambda to: pl.semaphore_signal(
-        barrier, inc=1, device_id={"row": to // cols, "col": lax.rem(to, cols)}, device_id_type=MESH))
+    others(parts, me, lambda to: pl.semaphore_signal(
+        barrier, inc=1, device_id={"row": to}, device_id_type=MESH))
+    others(cols, col, lambda to: pl.semaphore_signal(
+        barrier, inc=1, device_id={"col": to}, device_id_type=MESH))
     owner_copy = pltpu.make_async_copy(owner_hbm, owner_ref, owner_sem)
     owner_copy.start()
     row_copy = pltpu.make_async_copy(stored_ref, row_in, row_sem)
@@ -112,15 +112,52 @@
         odd = row_in[pl.ds(q + parts // 2, half, stride=parts), :]
         first_half = jnp.where(low_lanes, even, pltpu.roll(odd, BAND, 1))
         second_half = jnp.where(low_lanes, pltpu.roll(even, BAND, 1), odd)
-        send1[pl.ds(2 * q * cols, cols)] = first_half.reshape(cols, CHUNKS, LANES)
-        send1[pl.ds((2 * q + 1) * cols, cols)] = second_half.reshape(cols, CHUNKS, LANES)
-    recv1[mine] = send1[mine]
-
-    def copy1(to):
-        return pltpu.make_async_remote_copy(
-            src_ref=send1.at[to], dst_ref=recv1.at[mine], send_sem=s1, recv_sem=r1,
-            device_id={"row": to // cols, "col": lax.rem(to, cols)}, device_id_type=MESH,
-        )
+        for p, mixed in ((2 * q, first_half), (2 * q + 1, second_half)):
+            pieces = mixed.reshape(cols // 2, 2, CHUNKS, LANES)
+            send_a[p] = pieces[:, 0]
+            send_b[:, p] = pieces[:, 1]
+
+    odd = lax.rem(col, 2) == 1
+
+    def copy_a(to):
+        return pltpu.make_async_remote_copy(
+            src_ref=send_a.at[to], dst_ref=recv_a.at[me], send_sem=sa, recv_sem=ra,
+            device_id={"row": to}, device_id_type=MESH,
+        )
+
+    def copy_b(i):
+        return pltpu.make_async_remote_copy(
+            src_ref=send_b.at[i], dst_ref=recv_b.at[col], send_sem=sb.at[i], recv_sem=rb,
+            device_id={"col": 2 * i + 1}, device_id_type=MESH,
+        )
+
+    def pick_copy_a(i):
+        return pltpu.make_async_remote_copy(
+            src_ref=pick_a.at[i], dst_ref=from_a.at[col], send_sem=spa.at[i], recv_sem=rpa,
+            device_id={"col": 2 * i}, device_id_type=MESH,
+        )
+
+    def pick_copy_b(to):
+        return pltpu.make_async_remote_copy(
+            src_ref=pick_b.at[to], dst_ref=from_b.at[me], send_sem=spb, recv_sem=rpb,
+            device_id={"row": to}, device_id_type=MESH,
+        )
+
+    def each_other(parity, step):
+        def body(r, _):
+            i = lax.rem(col // 2 + r, cols // 2)
+
+            @pl.when(2 * i + parity != col)
+            def _():
+                step(i)
+
+            return 0
+
+        lax.fori_loop(0, cols // 2, body, 0)
+
+    def wait_for(ref, count, sem):
+        taken = ref.at[pl.ds(0, count)]
+        pltpu.make_async_copy(taken, taken, sem).wait()
 
     def copy3(to, source):
         return pltpu.make_async_remote_copy(
@@ -128,8 +165,15 @@
             device_id={"col": to}, device_id_type=MESH,
         )
 
-    pl.semaphore_wait(barrier, devices - 1)
-    others(devices, mine, lambda to: copy1(to).start())
+    pl.semaphore_wait(barrier, parts + cols - 2)
+    each_other(1, lambda i: copy_b(i).start())
+    others(parts, me, lambda to: copy_a(to).start())
+    recv_a[me] = send_a[me]
+
+    @pl.when(odd)
+    def _():
+        recv_b[col] = send_b[col // 2]
+
 
     rows = slab_in.shape[1]
 
@@ -148,10 +192,32 @@
     lax.fori_loop(0, cols, split_block, 0)
 
     owner_copy.wait()
-    every = recv1.at[pl.ds(0, devices - 1)]
-    pltpu.make_async_copy(every, every, r1).wait()
+    @pl.when(odd)
+    def _():
+        wait_for(recv_b, cols - 1, rb)
+        for g in range(GROUPS):
+            pick_b[:, g] = recv_b[lax.rem(owner_ref[g], cols)]
+        from_b[me] = pick_b[me]
+        others(parts, me, lambda to: pick_copy_b(to).start())
+
+    wait_for(recv_a, parts - 1, ra)
     for g in range(GROUPS):
-        recv3[col, g] = recv1[owner_ref[g]]
+        pick_a[:, g] = recv_a[owner_ref[g] // cols]
+    each_other(0, lambda i: pick_copy_a(i).start())
+
+    @pl.when(odd)
+    def _():
+        wait_for(from_b, parts - 1, rpb)
+        for g in range(GROUPS):
+            recv3[col, g] = from_b[owner_ref[g] // cols, g]
+
+    @pl.when(jnp.logical_not(odd))
+    def _():
+        from_a[col] = pick_a[col // 2]
+        wait_for(from_a, cols - 1, rpa)
+        for g in range(GROUPS):
+            recv3[col, g] = from_a[lax.rem(owner_ref[g], cols), g]
+
     others(cols, col, lambda to: copy3(to, col).start())
 
     lane8 = lax.broadcasted_iota(jnp.int32, (CHUNKS, LANES), 1)
@@ -336,8 +402,14 @@
             if g + 1 < GROUPS:
                 prepare(g + 1, n, q, par)
 
-    sent = send1.at[pl.ds(0, devices - 1)]
-    pltpu.make_async_copy(sent, sent, s1).wait()
+    wait_for(send_a, parts - 1, sa)
+    each_other(1, lambda i: copy_b(i).wait_send())
+    each_other(0, lambda i: pick_copy_a(i).wait_send())
+
+    @pl.when(odd)
+    def _():
+        wait_for(pick_b, parts - 1, spb)
+
     others(cols, col, lambda to: copy3(to, col).wait_send())
     for g in range(GROUPS):
         for n, q, par in steps:
@@ -370,8 +442,14 @@
             vmem(stored.shape, F32),
             vmem((cols, rows, WIDE), BF16),
             vmem((cols, rows, WIDE), BF16),
-            vmem((parts * cols, CHUNKS, LANES), F32),
-            vmem((parts * cols, CHUNKS, LANES), F32),
+            vmem((parts, cols // 2, CHUNKS, LANES), F32),
+            vmem((parts, cols // 2, CHUNKS, LANES), F32),
+            vmem((cols // 2, parts, CHUNKS, LANES), F32),
+            vmem((cols, parts, CHUNKS, LANES), F32),
+            vmem((cols // 2, GROUPS, CHUNKS, LANES), F32),
+            vmem((cols, GROUPS, CHUNKS, LANES), F32),
+            vmem((parts, GROUPS, CHUNKS, LANES), F32),
+            vmem((parts, GROUPS, CHUNKS, LANES), F32),
             vmem(piece, F32),
             vmem((4 * GROUPS, half, rows), F32),
             vmem((2, half, LANES), F32),
@@ -382,7 +460,8 @@
             vmem((GROUPS, blocks, 2, 2, half, LANES), F32),
             vmem((GROUPS, blocks, 2, 2, half, LANES), F32),
             dma, dma, dma((cols,)),
-            dma, dma,
+            dma, dma, dma((cols // 2,)), dma,
+            dma((cols // 2,)), dma, dma, dma,
             dma((cols,)), dma((cols,)),
             dma((2,)), dma((2,)),
             dma((GROUPS, blocks, 2, 2, PIECES)), dma((GROUPS, blocks, 2, 2, PIECES)),

time: 51.8 us -> 49.6 us (0.958)
  Pallas kernels: 51.6 us -> 49.5 us
    pallas_call x1, Pallas kernels: 46.7 us -> 44.5 us  [coefficients(): pl.pallas_call(functools.partial(coef_kernel, parts, cols), name='coeffic...]
where the time goes in v4:
time: 49.6 us; the launch traced here: 49.5 us
  Pallas kernels  49.5 us (100%)
    pallas_call x1, Pallas kernels, coefficients(): pl.pallas_call(functools.partial(coef_kernel, parts, cols), name='coeffic...  44.5 us
    pallas_call x1, Pallas kernels, update(): pl.pallas_call(functools.partial(update_kernel, cols), name='update', out...  4.92 us

profile of v4, /device:TPU:0, one launch (start us, length us, event | category | flops | bytes accessed | tf_op | source)
XLA Modules:
  0.0 49.5 jit_solution(14742091423414597715)
XLA Ops:
  0.0 44.5 %coefficients.1 = (f32[16,64,256]{2,1,0:T(8,128)S(1)}, f32[8,4,8,128]{3,2,1,0:T(8,128)S(1)}, f32[8,256,1024]{2,1,0:T(8,128)S(1)}) custom-call(s32[4]{0:T(128)} %owner_hbm.1, f32[1024,128]{1,0:T(8,128)} %bitcast.1, f32[256,8192]{1,0:T(8,128)} %slab_ref.1), custom_call_target="tpu_custom_call" | custom-call | tf_op jit(solution)/shard_map/coefficients/pallas_call | solution.py:426
  44.5 4.9 %update.1 = f32[256,8192]{1,0:T(8,128)} custom-call(f32[16,64,256]{2,1,0:T(8,128)S(1)} %get-tuple-element.8.coef_ref, f32[8,4,8,128]{3,2,1,0:T(8,128)S(1)} %get-tuple-element.9.vec_ref, f32[8,256,1024]{2,1,0:T(8,128)S(1)} %get-tuple-element.10.slab_ref), custom_call_target="tpu_custom_call" | custom-call | tf_op jit(solution)/shard_map/update/pallas_call | solution.py:512

commit v5 on v4

--- a/solution.py
+++ b/solution.py
@@ -12,6 +12,8 @@
 LANES = 128
 CHUNKS = 8
 WIDE = CHUNKS * LANES
+SUMS = 4 * GROUPS
+PAIR = 2 * LANES
 PIECES = 2
 MESH = pl.DeviceIdType.MESH
 F32 = jnp.float32
@@ -43,26 +45,33 @@
 
 
 def spread(vectors):
-    lane = lax.broadcasted_iota(jnp.int32, (CHUNKS, WIDE), 1)
-    row = lax.broadcasted_iota(jnp.int32, (CHUNKS, WIDE), 0)
-    here = (lane // LANES) == row
-    within = lane % LANES
-    zero = jnp.zeros((CHUNKS, WIDE), F32)
-    highs, lows = [], []
+    shape = (SUMS, LANES)
+    lane = lax.broadcasted_iota(jnp.int32, shape, 1)
+    line = lax.broadcasted_iota(jnp.int32, shape, 0)
+    group = line // 4
+    at = lane - BAND * lax.rem(line, 2)
+    keep = jnp.zeros(shape, jnp.bool_)
     for g in range(GROUPS):
-        v = vectors[g]
-        high = v.astype(BF16).astype(F32)
-        wide_high = jnp.concatenate([high] * CHUNKS, axis=1)
-        wide_low = jnp.concatenate([v - high] * CHUNKS, axis=1)
         for s in range(2):
             lo, hi = segment(g, s)
-            masks = [
-                here & (within >= BAND * par + lo) & (within < BAND * par + hi) for par in range(2)
-            ]
-            for wide, into in ((wide_high, highs), (wide_low, lows)):
-                both = jnp.concatenate([jnp.where(m, wide, zero) for m in masks], axis=0)
-                into.append(both.astype(BF16))
-    return jnp.concatenate(highs, axis=0), jnp.concatenate(lows, axis=0)
+            keep = keep | ((line // 2 == 2 * g + s) & (at >= lo) & (at < hi))
+    none = jnp.zeros(shape, BF16)
+    halves = []
+    for i in range(CHUNKS):
+        rows = [jnp.broadcast_to(vectors[g][i:i + 1, :], shape) for g in range(GROUPS)]
+        own = rows[0]
+        for g in range(1, GROUPS):
+            own = jnp.where(group == g, rows[g], own)
+        halves.append(split(jnp.where(keep, own, 0.0)))
+    pairs = []
+    for i in range(0, CHUNKS, 2):
+        first, second = halves[i], halves[i + 1]
+        lines = []
+        for term in range(2):
+            lines.append(jnp.concatenate([first[term], none], axis=1))
+            lines.append(jnp.concatenate([none, second[term]], axis=1))
+        pairs.append(jnp.concatenate(lines, axis=0))
+    return pairs
 
 
 def contract_lanes(a, b):
@@ -70,7 +79,7 @@
 
 
 def coef_kernel(
-    parts, cols, owner_hbm, stored_ref, slab_ref, coef_ref, vec_ref, slab_in,
+    parts, cols, owner_hbm, stored_ref, slab_ref, coef_ref, spread_ref, slab_in,
     owner_ref, row_in, high_in, low_in, send_a, recv_a, send_b, recv_b, pick_a, from_a, pick_b, from_b, recv3,
     raw, packed, square_out, square_in, gram, tau, send4, recv4,
     owner_sem, row_sem, slab_sem, sa, ra, sb, rb, spa, rpa, spb, rpb, s3, r3, st, rt, s4, r4,
@@ -87,6 +96,13 @@
             return 0
 
         lax.fori_loop(1, size, body, 0)
+
+    def farthest_first(fast, size, mine, step):
+        slow = size // fast
+        moves = [(a, b) for a in range(slow) for b in range(fast) if a or b]
+        moves.sort(key=lambda m: -(min(m[0], slow - m[0]) + min(m[1], fast - m[1])))
+        for a, b in moves:
+            step(lax.rem(mine // fast + a, slow) * fast + lax.rem(lax.rem(mine, fast) + b, fast))
 
     barrier = pltpu.get_barrier_semaphore()
     others(parts, me, lambda to: pl.semaphore_signal(
@@ -167,7 +183,7 @@
 
     pl.semaphore_wait(barrier, parts + cols - 2)
     each_other(1, lambda i: copy_b(i).start())
-    others(parts, me, lambda to: copy_a(to).start())
+    farthest_first(4, parts, me, lambda to: copy_a(to).start())
     recv_a[me] = send_a[me]
 
     @pl.when(odd)
@@ -198,7 +214,7 @@
         for g in range(GROUPS):
             pick_b[:, g] = recv_b[lax.rem(owner_ref[g], cols)]
         from_b[me] = pick_b[me]
-        others(parts, me, lambda to: pick_copy_b(to).start())
+        farthest_first(4, parts, me, lambda to: pick_copy_b(to).start())
 
     wait_for(recv_a, parts - 1, ra)
     for g in range(GROUPS):
@@ -218,7 +234,7 @@
         for g in range(GROUPS):
             recv3[col, g] = from_a[lax.rem(owner_ref[g], cols), g]
 
-    others(cols, col, lambda to: copy3(to, col).start())
+    farthest_first(2, cols, col, lambda to: copy3(to, col).start())
 
     lane8 = lax.broadcasted_iota(jnp.int32, (CHUNKS, LANES), 1)
 
@@ -232,14 +248,20 @@
         ]
 
     def partial(b):
+        for t, both in enumerate(spread(recv3[b])):
+            spread_ref[b, t] = both
+            lines = both.shape[0] // 2
+            at = slice(t * PAIR, (t + 1) * PAIR)
+            one = contract_lanes(both, high_in[b, :, at])
+            two = contract_lanes(both[:lines], low_in[b, :, at])
+            first = (b * CHUNKS + 2 * t) * SUMS
+            total = one[:lines] + (one[lines:] + two)
+            for n in range(rows // LANES):
+                raw[n, pl.ds(pl.multiple_of(first, 2 * SUMS), lines), :] = total[:, n * LANES:(n + 1) * LANES]
+
+    def square_sums(b):
         at = pl.ds(pl.multiple_of(b * CHUNKS, CHUNKS), CHUNKS)
         piece = recv3[b]
-        high, low = spread(piece)
-        depth = high.shape[0]
-        one = contract_lanes(jnp.concatenate([high, low], axis=0), high_in[b])
-        two = contract_lanes(high, low_in[b])
-        total = one[:depth] + (one[depth:] + two)
-        raw[:, at, :] = total.reshape(depth // CHUNKS, CHUNKS, total.shape[1])
         squares = [jnp.zeros((CHUNKS, LANES), F32) for _ in range(2)]
         for g in range(GROUPS):
             for s in range(2):
@@ -249,24 +271,32 @@
             packed[par, at, :] = squares[par]
 
     pair = (col // 2) * 2
-    copy3(lax.rem(col, 2) * -2 + 1 + col, lax.rem(col, 2) * -2 + 1 + col).wait_recv()
-    partial(pair)
-    partial(pair + 1)
-
-    def partial_pair(i, _):
-        src = lax.rem(pair + 2 * i, cols)
+    partner = pair + 1 - lax.rem(col, 2)
+    chips = cols // 2
+
+    def arrived(i):
+        away = jnp.where(lax.rem(i, 2) == 1, (i + 1) // 2, chips - i // 2)
+        src = lax.rem(pair + 2 * away, cols)
         copy3(src, src).wait_recv()
         copy3(src + 1, src + 1).wait_recv()
-        partial(src)
-        partial(src + 1)
-        return 0
-
-    lax.fori_loop(1, cols // 2, partial_pair, 0)
-
-    vec_ref[...] = recv3[...]
+        return src
+
+    def work(src):
+        for b in (src, src + 1):
+            square_sums(b)
+        for b in (src, src + 1):
+            partial(b)
+
+    copy3(partner, partner).wait_recv()
+    final = pair
+    if chips > 1:
+        work(pair)
+        lax.fori_loop(1, chips - 1, lambda i, _: (work(arrived(i)), 0)[1], 0)
+        final = arrived(jnp.int32(chips - 1))
+    square_sums(final)
+    square_sums(final + 1)
     vectors = [recv3[:, g].reshape(half, LANES) for g in range(GROUPS)]
     lane = lax.broadcasted_iota(jnp.int32, (half, LANES), 1)
-
     square_out[...] = jnp.concatenate([packed[0], packed[1]], axis=0).T[:2 * GROUPS, :]
 
     def square_copy(way, to):
@@ -278,6 +308,8 @@
     square_copies = [square_copy(0, left), square_copy(1, right)]
     for c in square_copies:
         c.start()
+    partial(final)
+    partial(final + 1)
 
     blocks = rows // LANES
     part = half // PIECES
@@ -294,14 +326,16 @@
             device_id={"row": to}, device_id_type=MESH,
         )
 
+    def line(q, g, s, par):
+        return pl.ds(q * part * SUMS + 4 * g + 2 * s + par, part, stride=SUMS)
+
     def prepare(g, n, q, par):
-        at = pl.ds(n * LANES, LANES)
         tiles = pl.ds(q * part, part)
         for s in range(2):
-            x = raw[4 * g + 2 * s + par, tiles, at]
+            x = raw[n, line(q, g, s, par), :]
             for k, (pg, ps, h, t, _, _) in enumerate(PAIRS):
                 if (pg, ps) == (g, s):
-                    x = x - gram[k, par, tiles] * coef_ref[4 * h + 2 * t + par, tiles, at]
+                    x = x - gram[k, par, tiles] * coef_ref[n, line(q, h, t, par), :]
             send4[g, n, s, par, tiles] = x
         exchange(g, n, 0, par, q).start()
         exchange(g, n, 1, par, q).start()
@@ -356,13 +390,12 @@
         return lax.cond(first, shifted, lambda: from_ref[q * part:(q + 1) * part])
 
     def finish(g, n, q, par):
-        at = pl.ds(n * LANES, LANES)
         tiles = pl.ds(q * part, part)
         after = heads_after(g, n, q, par)
         before = tails_before(g, n, q, par)
         head, tail = send4[g, n, 0, par, tiles], send4[g, n, 1, par, tiles]
-        coef_ref[4 * g + par, tiles, at] = tau[2 * g, par, tiles] * (before + head)
-        coef_ref[4 * g + 2 + par, tiles, at] = tau[2 * g + 1, par, tiles] * (tail + after)
+        coef_ref[n, line(q, g, 0, par), :] = tau[2 * g, par, tiles] * (before + head)
+        coef_ref[n, line(q, g, 1, par), :] = tau[2 * g + 1, par, tiles] * (tail + after)
 
     for n, q, par in steps:
         prepare(0, n, q, par)
@@ -427,8 +460,8 @@
         functools.partial(coef_kernel, parts, cols),
         name="coefficients",
         out_shape=(
-            jax.ShapeDtypeStruct((4 * GROUPS, half, rows), F32),
-            jax.ShapeDtypeStruct(piece, F32),
+            jax.ShapeDtypeStruct((blocks, half * SUMS, LANES), F32),
+            jax.ShapeDtypeStruct((cols, CHUNKS // 2, 4 * SUMS, PAIR), BF16),
             jax.ShapeDtypeStruct((cols, rows, WIDE), F32),
         ),
         in_specs=[
@@ -451,7 +484,7 @@
             vmem((parts, GROUPS, CHUNKS, LANES), F32),
             vmem((parts, GROUPS, CHUNKS, LANES), F32),
             vmem(piece, F32),
-            vmem((4 * GROUPS, half, rows), F32),
+            vmem((blocks, half * SUMS, LANES), F32),
             vmem((2, half, LANES), F32),
             vmem((2 * GROUPS, 2 * half), F32),
             vmem((2, 2 * GROUPS, 2 * half), F32),
@@ -472,7 +505,7 @@
     )(*(pltpu.with_memory_space_constraint(x, pltpu.HBM) for x in (owner, stored, slab)))
 
 
-def update_kernel(cols, coef_ref, vec_ref, slab_ref, out_ref, ready, sem):
+def update_kernel(cols, coef_ref, spread_ref, slab_ref, out_ref, ready, sem):
     slots = ready.shape[0]
 
     def copy(b):
@@ -481,15 +514,23 @@
         return pltpu.make_async_copy(ready.at[slot], out_ref.at[:, at], sem.at[slot])
 
     def block(b):
-        coef = coef_ref[:, pl.ds(pl.multiple_of(b * CHUNKS, CHUNKS), CHUNKS), :]
-        turned = coef.reshape(coef.shape[0] * coef.shape[1], coef.shape[2]).T
-        high, low = split(turned)
-        thigh, tlow = spread(vec_ref[b])
-        change = jnp.dot(
-            jnp.concatenate([high, high], axis=1), jnp.concatenate([tlow, thigh], axis=0),
-            preferred_element_type=F32,
-        ) + jnp.dot(low, thigh, preferred_element_type=F32)
-        ready[lax.rem(b, slots)] = slab_ref[b] - change
+        lines = CHUNKS * SUMS
+        at = pl.ds(pl.multiple_of(b * lines, lines), lines)
+        high, low = split(jnp.concatenate([coef_ref[n, at, :] for n in range(coef_ref.shape[0])], axis=1))
+        stack = []
+        for t in range(CHUNKS // 2):
+            at = slice(t * 2 * SUMS, (t + 1) * 2 * SUMS)
+            stack += [high[at], high[at], low[at], low[at]]
+        turned = jnp.concatenate(stack, axis=0).T
+        for t in range(CHUNKS // 2):
+            both = spread_ref[b, t]
+            depth = 2 * both.shape[0]
+            change = jnp.dot(
+                turned[:, t * depth:(t + 1) * depth], jnp.concatenate([both, both], axis=0),
+                preferred_element_type=F32,
+            )
+            at = slice(t * PAIR, (t + 1) * PAIR)
+            ready[lax.rem(b, slots), :, at] = slab_ref[b, :, at] - change
 
     def two(i, _):
         @pl.when(i >= slots // 2)
@@ -498,8 +539,8 @@
             copy(2 * i + 1 - slots).wait()
 
         block(2 * i)
+        copy(2 * i).start()
         block(2 * i + 1)
-        copy(2 * i).start()
         copy(2 * i + 1).start()
         return 0
 
@@ -507,22 +548,22 @@
     lax.fori_loop(max(cols - slots, 0), cols, lambda b, _: (copy(b).wait(), 0)[1], 0)
 
 
-def update(cols, coef, vec, slab_in):
-    blocks, rows, wide = slab_in.shape
+def update(cols, coef, wide, slab_in):
+    blocks, rows, length = slab_in.shape
     return pl.pallas_call(
         functools.partial(update_kernel, cols),
         name="update",
-        out_shape=jax.ShapeDtypeStruct((rows, blocks * wide), F32),
+        out_shape=jax.ShapeDtypeStruct((rows, blocks * length), F32),
         in_specs=[pl.BlockSpec(memory_space=pltpu.VMEM)] * 3,
         out_specs=pl.BlockSpec(memory_space=pltpu.HBM),
-        scratch_shapes=[pltpu.VMEM((4, rows, wide), F32), pltpu.SemaphoreType.DMA((4,))],
+        scratch_shapes=[pltpu.VMEM((4, rows, length), F32), pltpu.SemaphoreType.DMA((4,))],
         compiler_params=pltpu.CompilerParams(vmem_limit_bytes=24 * 1024 * 1024),
-    )(coef, vec, slab_in)
+    )(coef, wide, slab_in)
 
 
 def shards(parts, cols, slab, stored, owner):
-    coef, vec, slab_in = coefficients(parts, cols, owner, stored.reshape(-1, LANES), slab)
-    return update(cols, coef, vec, slab_in)
+    coef, wide, slab_in = coefficients(parts, cols, owner, stored.reshape(-1, LANES), slab)
+    return update(cols, coef, wide, slab_in)
 
 
 def solution(mesh):

time: 49.6 us -> 47.7 us (0.962)
  Pallas kernels: 49.5 us -> 47.6 us
    pallas_call x1, Pallas kernels: 4.92 us -> 4 us  [update(): pl.pallas_call(functools.partial(update_kernel, cols), name='update', out...]
    pallas_call x1, Pallas kernels: 44.5 us -> 43.6 us  [coefficients(): pl.pallas_call(functools.partial(coef_kernel, parts, cols), name='coeffic...]
where the time goes in v5:
time: 47.7 us; the launch traced here: 47.6 us
  Pallas kernels  47.6 us (100%)
    pallas_call x1, Pallas kernels, coefficients(): pl.pallas_call(functools.partial(coef_kernel, parts, cols), name='coeffic...  43.6 us
    pallas_call x1, Pallas kernels, update(): pl.pallas_call(functools.partial(update_kernel, cols), name='update', out...  4 us

profile of v5, /device:TPU:0, one launch (start us, length us, event | category | flops | bytes accessed | tf_op | source)
XLA Modules:
  0.0 47.6 jit_solution(6003834135158251716)
XLA Ops:
  0.0 43.6 %coefficients.1 = (f32[2,1024,128]{2,1,0:T(8,128)S(1)}, bf16[8,4,64,256]{3,2,1,0:T(8,128)(2,1)S(1)}, f32[8,256,1024]{2,1,0:T(8,128)S(1)}) custom-call(s32[4]{0:T(128)} %owner_hbm.1, f32[1024,128]{1,0:T(8,128)} %bitcast.1, f32[256,8192]{1,0:T(8,128)} %slab_ref.1), custom_call_target="tpu_custom_call" | custom-call | tf_op jit(solution)/shard_map/coefficients/pallas_call | solution.py:459
  43.7 4.0 %update.1 = f32[256,8192]{1,0:T(8,128)} custom-call(f32[2,1024,128]{2,1,0:T(8,128)S(1)} %get-tuple-element.8.coef_ref, bf16[8,4,64,256]{3,2,1,0:T(8,128)(2,1)S(1)} %get-tuple-element.9.spread_ref, f32[8,256,1024]{2,1,0:T(8,128)S(1)} %get-tuple-element.10.slab_ref), custom_call_target="tpu_custom_call" | custom-call | tf_op jit(solution)/shard_map/update/pallas_call | solution.py:553

commit v6 on v5

--- a/solution.py
+++ b/solution.py
@@ -182,8 +182,8 @@
         )
 
     pl.semaphore_wait(barrier, parts + cols - 2)
+    farthest_first(4, parts, me, lambda to: copy_a(to).start())
     each_other(1, lambda i: copy_b(i).start())
-    farthest_first(4, parts, me, lambda to: copy_a(to).start())
     recv_a[me] = send_a[me]
 
     @pl.when(odd)

time: 47.7 us -> 47.8 us (level)
  no operation moved by 1% of the time
where the time goes in v6:
time: 47.8 us; the launch traced here: 47.7 us
  Pallas kernels  47.6 us (100%)
    pallas_call x1, Pallas kernels, coefficients(): pl.pallas_call(functools.partial(coef_kernel, parts, cols), name='coeffic...  43.6 us
    pallas_call x1, Pallas kernels, update(): pl.pallas_call(functools.partial(update_kernel, cols), name='update', out...  4 us

profile of v6, /device:TPU:0, one launch (start us, length us, event | category | flops | bytes accessed | tf_op | source)
XLA Modules:
  0.0 47.7 jit_solution(1643041967330160419)
XLA Ops:
  0.0 43.6 %coefficients.1 = (f32[2,1024,128]{2,1,0:T(8,128)S(1)}, bf16[8,4,64,256]{3,2,1,0:T(8,128)(2,1)S(1)}, f32[8,256,1024]{2,1,0:T(8,128)S(1)}) custom-call(s32[4]{0:T(128)} %owner_hbm.1, f32[1024,128]{1,0:T(8,128)} %bitcast.1, f32[256,8192]{1,0:T(8,128)} %slab_ref.1), custom_call_target="tpu_custom_call" | custom-call | tf_op jit(solution)/shard_map/coefficients/pallas_call | solution.py:459
  43.7 4.0 %update.1 = f32[256,8192]{1,0:T(8,128)} custom-call(f32[2,1024,128]{2,1,0:T(8,128)S(1)} %get-tuple-element.8.coef_ref, bf16[8,4,64,256]{3,2,1,0:T(8,128)(2,1)S(1)} %get-tuple-element.9.spread_ref, f32[8,256,1024]{2,1,0:T(8,128)S(1)} %get-tuple-element.10.slab_ref), custom_call_target="tpu_custom_call" | custom-call | tf_op jit(solution)/shard_map/update/pallas_call | solution.py:553

commit v7 on v5

--- a/solution.py
+++ b/solution.py
@@ -14,6 +14,7 @@
 WIDE = CHUNKS * LANES
 SUMS = 4 * GROUPS
 PAIR = 2 * LANES
+OUT_CUTS = 2
 PIECES = 2
 MESH = pl.DeviceIdType.MESH
 F32 = jnp.float32
@@ -160,16 +161,13 @@
         )
 
     def each_other(parity, step):
-        def body(r, _):
-            i = lax.rem(col // 2 + r, cols // 2)
-
-            @pl.when(2 * i + parity != col)
-            def _():
+        chips = cols // 2
+        for r in sorted(range(chips), key=lambda r: -min(r, chips - r)):
+            i = lax.rem(col // 2 + r, chips)
+            if r:
                 step(i)
-
-            return 0
-
-        lax.fori_loop(0, cols // 2, body, 0)
+            else:
+                pl.when(2 * i + parity != col)(functools.partial(step, i))
 
     def wait_for(ref, count, sem):
         taken = ref.at[pl.ds(0, count)]
@@ -508,10 +506,21 @@
 def update_kernel(cols, coef_ref, spread_ref, slab_ref, out_ref, ready, sem):
     slots = ready.shape[0]
 
-    def copy(b):
+    rows = ready.shape[1] // OUT_CUTS
+
+    def cut(b, k):
         slot = lax.rem(b, slots)
         at = pl.ds(pl.multiple_of(b * WIDE, WIDE), WIDE)
-        return pltpu.make_async_copy(ready.at[slot], out_ref.at[:, at], sem.at[slot])
+        some = pl.ds(k * rows, rows)
+        return pltpu.make_async_copy(ready.at[slot, some], out_ref.at[some, at], sem.at[slot, k])
+
+    def start(b):
+        for k in range(OUT_CUTS):
+            cut(b, k).start()
+
+    def wait(b):
+        for k in range(OUT_CUTS):
+            cut(b, k).wait()
 
     def block(b):
         lines = CHUNKS * SUMS
@@ -535,17 +544,17 @@
     def two(i, _):
         @pl.when(i >= slots // 2)
         def _():
-            copy(2 * i - slots).wait()
-            copy(2 * i + 1 - slots).wait()
+            wait(2 * i - slots)
+            wait(2 * i + 1 - slots)
 
         block(2 * i)
-        copy(2 * i).start()
+        start(2 * i)
         block(2 * i + 1)
-        copy(2 * i + 1).start()
+        start(2 * i + 1)
         return 0
 
     lax.fori_loop(0, cols // 2, two, 0)
-    lax.fori_loop(max(cols - slots, 0), cols, lambda b, _: (copy(b).wait(), 0)[1], 0)
+    lax.fori_loop(max(cols - slots, 0), cols, lambda b, _: (wait(b), 0)[1], 0)
 
 
 def update(cols, coef, wide, slab_in):
@@ -556,7 +565,7 @@
         out_shape=jax.ShapeDtypeStruct((rows, blocks * length), F32),
         in_specs=[pl.BlockSpec(memory_space=pltpu.VMEM)] * 3,
         out_specs=pl.BlockSpec(memory_space=pltpu.HBM),
-        scratch_shapes=[pltpu.VMEM((4, rows, length), F32), pltpu.SemaphoreType.DMA((4,))],
+        scratch_shapes=[pltpu.VMEM((4, rows, length), F32), pltpu.SemaphoreType.DMA((4, OUT_CUTS))],
         compiler_params=pltpu.CompilerParams(vmem_limit_bytes=24 * 1024 * 1024),
     )(coef, wide, slab_in)
 

time: 47.7 us -> 48 us (level)
  no operation moved by 1% of the time
where the time goes in v7:
time: 48 us; the launch traced here: 47.9 us
  Pallas kernels  47.9 us (100%)
    pallas_call x1, Pallas kernels, coefficients(): pl.pallas_call(functools.partial(coef_kernel, parts, cols), name='coeffic...  43.9 us
    pallas_call x1, Pallas kernels, update(): pl.pallas_call(functools.partial(update_kernel, cols), name='update', out...  4.01 us

profile of v7, /device:TPU:0, one launch (start us, length us, event | category | flops | bytes accessed | tf_op | source)
XLA Modules:
  0.0 47.9 jit_solution(2126189779810053785)
XLA Ops:
  0.0 43.9 %coefficients.1 = (f32[2,1024,128]{2,1,0:T(8,128)S(1)}, bf16[8,4,64,256]{3,2,1,0:T(8,128)(2,1)S(1)}, f32[8,256,1024]{2,1,0:T(8,128)S(1)}) custom-call(s32[4]{0:T(128)} %owner_hbm.1, f32[1024,128]{1,0:T(8,128)} %bitcast.1, f32[256,8192]{1,0:T(8,128)} %slab_ref.1), custom_call_target="tpu_custom_call" | custom-call | tf_op jit(solution)/shard_map/coefficients/pallas_call | solution.py:457
  43.9 4.0 %update.1 = f32[256,8192]{1,0:T(8,128)} custom-call(f32[2,1024,128]{2,1,0:T(8,128)S(1)} %get-tuple-element.8.coef_ref, bf16[8,4,64,256]{3,2,1,0:T(8,128)(2,1)S(1)} %get-tuple-element.9.spread_ref, f32[8,256,1024]{2,1,0:T(8,128)S(1)} %get-tuple-element.10.slab_ref), custom_call_target="tpu_custom_call" | custom-call | tf_op jit(solution)/shard_map/update/pallas_call | solution.py:562
